TPU v7x, 32 devices: a whole 2x2x4 slice. The times are simulated.
32 devices in a mesh: seg: 8 (over z, x), par: 4 (over y, core).
Axes of the slice: x: 2, y: 2, z: 4, core: 2. Of those that a mesh axis runs over, the one named last changes fastest.
Arguments:
- points: bfloat16 [64, 128, 16384], P('seg', 'par'), may hold values from -9 to 9
- source_segment: int32 [64], P('seg'), may hold values from 0 to 62, as said below
- numerators: int32 [64], P('seg'), may hold values from 0 to 65535
Outputs:
- resampled: bfloat16 [64, 128, 16384], P('seg', 'par')
- arc: float32 [64], P('seg')
Inputs may be any that keep to these rules, and one draw needn't show every extreme that they name: j - 3 <= source_segment[j] <= j + 2.
All inputs are finite; a program needn't handle non-finite values.
Results may differ from a plain program's by a relative error of at most 0.0017.
Values may be sent and summed in bfloat16 or wider, within the bound.
No kernel may reach another device: no remote copies, remote signals or barrier semaphores. Data moves between devices by JAX's collectives and lax.ppermute only.
A program may use at most 128 MiB of HBM per device.

v0:
```python
import jax
import jax.numpy as jnp
from jax import lax
from jax.sharding import PartitionSpec as P


def padded_2(block, sides, width):
    for axis, dim in sides:
        count = lax.axis_size(axis)
        forward = [(i, i + 1) for i in range(count - 1)]
        backward = [(target, source) for source, target in forward]
        low = lax.ppermute(
            lax.slice_in_dim(block, block.shape[dim] - width, None, axis=dim), axis, forward
        )
        high = lax.ppermute(lax.slice_in_dim(block, 0, width, axis=dim), axis, backward)
        block = jnp.concatenate([low, block, high], axis=dim)
    return block


def squares(blocks, following):
    difference = following.astype(jnp.float32) - blocks.astype(jnp.float32)
    return jnp.sum(difference * difference, axis=(1, 2))


def chain_offsets(own_sum, device_index):
    device_sums = lax.all_gather(own_sum.reshape(1), "seg", axis=0, tiled=True)
    positions = jnp.arange(device_sums.shape[0], dtype=jnp.int32)
    offset_arc = jnp.sum(jnp.where(positions < device_index, device_sums, 0.0))
    total_length = jnp.sum(device_sums)
    return (offset_arc, total_length)


def per_device(points, source_segment, numerators):
    local_points = points.shape[0]
    device_index = lax.axis_index("seg")
    device_count = lax.axis_size("seg")
    first_point = device_index * local_points
    point_count = device_count * local_points
    padded = padded_2(points, (("seg", 0),), 3)
    segment_ids = jnp.arange(local_points + 5, dtype=jnp.int32) + first_point - 3
    in_range = (segment_ids >= 0) & (segment_ids <= point_count - 2)
    buffer_rows = source_segment - first_point + 3
    targets_scale = (
        source_segment.astype(jnp.float32) + numerators.astype(jnp.float32) / 65536.0
    ) / (point_count - 1)
    partial_sums = squares(padded[:-1], padded[1:])
    total_squares = lax.psum(partial_sums, "par")
    lengths = jnp.where(in_range, jnp.sqrt(total_squares), 0.0)
    own_sum = jnp.sum(lengths[3 : 3 + local_points])
    offset_arc, total_length = chain_offsets(own_sum, device_index)
    running_sum = jnp.concatenate([jnp.zeros((1,), jnp.float32), jnp.cumsum(lengths)])
    arcs_wide = offset_arc + (running_sum - running_sum[3])
    fraction = (total_length * targets_scale - arcs_wide[buffer_rows]) / lengths[buffer_rows]
    arc = arcs_wide[3 : 3 + local_points] / total_length
    start_rows = padded[buffer_rows].astype(jnp.float32)
    end_rows = padded[buffer_rows + 1].astype(jnp.float32)
    resampled = (start_rows + fraction[:, None, None] * (end_rows - start_rows)).astype(
        jnp.bfloat16
    )
    return (resampled, arc)


def solution(mesh):
    in_specs = (P("seg", "par", None), P("seg"), P("seg"))
    out_specs = (P("seg", "par", None), P("seg"))
    return jax.shard_map(
        per_device, mesh=mesh, in_specs=in_specs, out_specs=out_specs, check_vma=False
    )
```

profile of v0, /device:TPU:0, one launch (start us, length us, event | category | flops | bytes accessed | tf_op | source)
XLA Modules:
  0.0 235.8 jit_solution(3718425185802364838)
XLA Ops:
  0.6 6.2 %fusion.5 = (bf16[3,32,16384]{2,1,0:T(8,128)(2,1)}, bf16[3,32,16384]{2,1,0:T(8,128)(2,1)}) fusion(bf16[8,32,16384]{2,1,0:T(8,128)(2,1)} %param.3), kind=kLoop, calls=%fused_computation.28 | loop fusion | bytes 12582912 | tf_op jit(solution)/shard_map/slice | solution.py:15
  6.8 6.5 %collective-permute-start = (bf16[3,32,16384]{2,1,0:T(8,128)(2,1)}, bf16[3,32,16384]{2,1,0:T(8,128)(2,1)}, u32[]{:S(2)}, u32[]{:S(2)}) collective-permute-start(bf16[3,32,16384]{2,1,0:T(8,128)(2,1)} %get-tuple-element.5), channel_id=1, source_target_pairs={{0,4},{4,8},{8,12},{12,16},{16,20},{20,24},{24,28},{1,5},{5,9},{9,... | collective-permute-start | bytes 9437192 | tf_op jit(solution)/shard_map/ppermute | solution.py:12
  13.3 1.3 collective-permute-start.1
  14.6 1.2 dynamic-slice
  15.8 0.7 compare_select_fusion
  16.5 130.2 %collective-permute-done = bf16[3,32,16384]{2,1,0:T(8,128)(2,1)} collective-permute-done((bf16[3,32,16384]{2,1,0:T(8,128)(2,1)}, bf16[3,32,16384]{2,1,0:T(8,128)(2,1)}, u32[]{:S(2)}, u32[]{:S(2)}) %collective-permute-start) | collective-permute-done | bytes 3145760 | tf_op jit(solution)/shard_map/ppermute | solution.py:12
  146.7 3.8 %constant_dynamic-update-slice_fusion.2 = bf16[14,32,16384]{2,1,0:T(8,128)(2,1)} fusion(bf16[3,32,16384]{2,1,0:T(8,128)(2,1)} %collective-permute-done), kind=kLoop, calls=%fused_computation.11 | loop fusion | bytes 6291456
  150.5 7.7 %constant_dynamic-update-slice_fusion.1 = bf16[14,32,16384]{2,1,0:T(8,128)(2,1)} fusion(bf16[14,32,16384]{2,1,0:T(8,128)(2,1)} %constant_dynamic-update-slice_fusion.2, bf16[8,32,16384]{2,1,0:T(8,128)(2,1)} %param.3), kind=kLoop, calls=%fused_computation.10 | loop fusion | bytes 16777216
  158.1 0.0 collective-permute-done.1
  158.1 2.0 constant_dynamic-update-slice_fusion
  160.1 12.0 %multiply_reduce_fusion = f32[13]{0:T(128)S(1)} fusion(bf16[14,32,16384]{2,1,0:T(8,128)(2,1)} %constant_dynamic-update-slice_fusion), kind=kLoop, calls=%fused_computation.4 | loop fusion | flops 34078708 | bytes 27263028 | tf_op jit(solution)/shard_map/reduce_sum | solution.py:22
  172.1 5.7 %psum.7 = f32[13]{0:T(128)S(1)} all-reduce(f32[13]{0:T(128)S(1)} %multiply_reduce_fusion), channel_id=1, replica_groups=mesh['seg'=8,'par'=4] {'par'}, use_global_device_ids=true, to_apply=%region_1.0 | all-reduce | flops 13 | bytes 104 | tf_op jit(solution)/shard_map/psum | solution.py:47
  177.8 0.7 slice_reduce_fusion
  178.5 1.3 dynamic-update-slice
  179.8 19.8 %all-reduce = f32[8]{0:T(128)S(1)} all-reduce(f32[8]{0:T(128)S(1)} %dynamic-update-slice), channel_id=1, replica_groups=mesh['seg'=8,'par'=4] {'seg'}, use_global_device_ids=true, to_apply=%add | all-reduce | flops 8 | bytes 64
  199.6 0.7 fusion.4
  200.3 0.2 reduce-window.4
  200.5 0.6 slice.27
  201.1 0.0 copy-start
  201.1 0.0 copy-start.1
  201.1 10.0 %gather_fusion = bf16[8,32,16384]{2,1,0:T(8,128)(2,1)} fusion(bf16[14,32,16384]{2,1,0:T(8,128)(2,1)} %constant_dynamic-update-slice_fusion, s32[1024]{0:T(1024)S(1)} %get-tuple-element.10), kind=kCustom, calls=%fused_computation | custom fusion | bytes 16777248 | tf_op jit(solution)/shard_map/gather | solution.py:55
  211.1 1.4 fusion.3
  212.5 0.6 gather_fusion.1
  213.2 0.6 gather_fusion.2
  213.8 1.2 slice_divide_fusion
  215.7 9.9 %gather_fusion.3 = bf16[8,32,16384]{2,1,0:T(8,128)(2,1)} fusion(bf16[14,32,16384]{2,1,0:T(8,128)(2,1)} %constant_dynamic-update-slice_fusion, s32[1024]{0:T(1024)S(1)} %get-tuple-element.9), kind=kCustom, calls=%fused_computation.3 | custom fusion | bytes 16777248 | tf_op jit(solution)/shard_map/gather | solution.py:56
  225.6 0.0 copy-done
  225.6 0.0 copy-done.1
  225.6 10.2 %fusion.1 = bf16[8,32,16384]{2,1,0:T(8,128)(2,1)} fusion(bf16[8,32,16384]{2,1,0:T(8,128)(2,1)} %gather_fusion, bf16[8,32,16384]{2,1,0:T(8,128)(2,1)} %gather_fusion.3, f32[8]{0:T(128)S(1)} %subtract_divide_fusion), kind=kLoop, calls=%fused_computation.8 | loop fusion | flops 25165824 | bytes 25165856 | tf_op jit(solution)/shard_map/convert_element_type | solution.py:57
  (6 shorter events, 0.0 us)
Async XLA Ops:
  6.8 139.9 %collective-permute-start = (bf16[3,32,16384]{2,1,0:T(8,128)(2,1)}, bf16[3,32,16384]{2,1,0:T(8,128)(2,1)}, u32[]{:S(2)}, u32[]{:S(2)}) collective-permute-start(bf16[3,32,16384]{2,1,0:T(8,128)(2,1)} %get-tuple-element.5), channel_id=1, source_target_pairs={{0,4},{4,8},{8,12},{12,16},{16,20},{20,24},{24,28},{1,5},{5,9},{9,... | collective-permute-start | bytes 9437192 | tf_op jit(solution)/shard_map/ppermute | solution.py:12
  13.3 144.9 %collective-permute-start.1 = (bf16[3,32,16384]{2,1,0:T(8,128)(2,1)}, bf16[3,32,16384]{2,1,0:T(8,128)(2,1)S(1)}, u32[]{:S(2)}, u32[]{:S(2)}) collective-permute-start(bf16[3,32,16384]{2,1,0:T(8,128)(2,1)} %get-tuple-element.4), channel_id=1, source_target_pairs={{4,0},{8,4},{12,8},{16,12},{20,16},{24,20},{28,24},{5,1},{9,5},{13... | collective-permute-start | bytes 9437192 | tf_op jit(solution)/shard_map/ppermute | solution.py:15
  201.1 24.5 %copy-start = (s32[8]{0:T(128)S(1)}, s32[8]{0:T(128)}, u32[]{:S(2)}) copy-start(s32[8]{0:T(128)} %param.4) | copy-start | bytes 100
  201.1 24.5 %copy-start.1 = (s32[8]{0:T(128)S(1)}, s32[8]{0:T(128)}, u32[]{:S(2)}) copy-start(s32[8]{0:T(128)} %param.5) | copy-start | bytes 100
where the time goes:
time: 236 us
  waiting for transfers between devices  130 us (55%)
  local copies, waits for them, and re-layouts  43.9 us (19%)
  other arithmetic  27.1 us (11%)
  blocking collectives  25.6 us (11%)
  starting transfers between devices  7.77 us (3%)
    ppermute x1, waiting for transfers between devices, padded_2(): lax.ppermute(lax.slice_in_dim(block, block.shape[dim] - width, None, axis...  130 us
    unnamed x1, blocking collectives  19.8 us
    unnamed x9, local copies, waits for them, and re-layouts  14 us
    reduce_sum x1, other arithmetic, squares(): return jnp.sum(difference * difference, axis=(1, 2))  12 us
    convert_element_type x1, other arithmetic, per_device(): (start_rows + fraction[:, None, None] * (end_rows - start_rows)).astype(j...  10.2 us
    gather x1, local copies, waits for them, and re-layouts, per_device(): start_rows = padded[buffer_rows].astype(jnp.float32)  10 us
    gather x1, local copies, waits for them, and re-layouts, per_device(): end_rows = padded[buffer_rows + 1].astype(jnp.float32)  9.91 us
    ppermute x1, starting transfers between devices, padded_2(): lax.ppermute(lax.slice_in_dim(block, block.shape[dim] - width, None, axis...  6.49 us
  transfers between devices with their start and end apart: 2, of which 1 were waited for; matrix products, arithmetic and copies ran while one was open for 6% of the time, Pallas kernels for 0%

commit v1 on v0

v1 whole, which is shorter than its diff:
```python
import functools

import jax
import jax.numpy as jnp
from jax import lax
from jax.experimental import pallas as pl
from jax.experimental.pallas import tpu as pltpu
from jax.sharding import PartitionSpec as P


TILE_ROWS = 8
COL_BLOCKS = 4
LOW = 3


def place_kernel(
    chunk, n_own, rows, has_prev,
    buffer_rows, fractions, points, first, low, high, *rest
):
    if has_prev:
        rest = rest[1:]
    out, buf, res, in_sem, out_sem = rest
    width = points.shape[2]
    cols = width // COL_BLOCKS
    row0 = chunk * rows
    n_high = high.shape[0]

    def in_copies(c):
        at = pl.ds(c * cols, cols)
        own = pl.ds(row0, rows)
        pairs = (
            (points.at[:, own, at], buf.at[pl.ds(LOW, n_own), :, at]),
            (first.at[:, own, at], buf.at[pl.ds(LOW + n_own, 1), :, at]),
            (low.at[:, :, at], buf.at[pl.ds(0, LOW), :, at]),
            (high.at[:, :, at], buf.at[pl.ds(LOW + n_own + 1, n_high), :, at]),
        )
        return [
            pltpu.make_async_copy(src, dst, in_sem.at[c, k])
            for k, (src, dst) in enumerate(pairs)
        ]

    def out_copy(c):
        at = pl.ds(c * cols, cols)
        return pltpu.make_async_copy(
            res.at[:, :, at], out.at[:, pl.ds(row0, rows), at], out_sem.at[c]
        )

    for c in range(COL_BLOCKS):
        for copy in in_copies(c):
            copy.start()
    for c in range(COL_BLOCKS):
        for copy in in_copies(c):
            copy.wait()
        at = pl.ds(c * cols, cols)

        @pl.loop(0, n_own)
        def _(j):
            start = buf[buffer_rows[j], :, at].astype(jnp.float32)
            end = buf[buffer_rows[j] + 1, :, at].astype(jnp.float32)
            res[j, :, at] = (start + fractions[j] * (end - start)).astype(res.dtype)

        out_copy(c).start()
    for c in range(COL_BLOCKS):
        out_copy(c).wait()


def place(chunk, rows, buffer_rows, fractions, points, first, low, high, prev):
    n_own, _, width = points.shape
    held = LOW + n_own + 1 + high.shape[0]
    hbm = pl.BlockSpec(memory_space=pl.ANY)
    smem = pl.BlockSpec(memory_space=pltpu.SMEM)
    args = [buffer_rows, fractions, points, first, low, high]
    if prev is not None:
        args.append(prev)
    moved = (held + n_own) * rows * width * points.dtype.itemsize
    return pl.pallas_call(
        functools.partial(place_kernel, chunk, n_own, rows, prev is not None),
        out_shape=jax.ShapeDtypeStruct(points.shape, points.dtype),
        in_specs=[smem, smem] + [hbm] * (len(args) - 2),
        out_specs=hbm,
        scratch_shapes=[
            pltpu.VMEM((held, rows, width), points.dtype),
            pltpu.VMEM((n_own, rows, width), points.dtype),
            pltpu.SemaphoreType.DMA((COL_BLOCKS, 4)),
            pltpu.SemaphoreType.DMA((COL_BLOCKS,)),
        ],
        input_output_aliases={} if prev is None else {len(args) - 1: 0},
        cost_estimate=pl.CostEstimate(
            flops=4 * n_own * rows * width, bytes_accessed=moved, transcendentals=0
        ),
    )(*args)


def per_device(points, source_segment, numerators):
    n_own, n_rows, _ = points.shape
    device_index = lax.axis_index("seg")
    device_count = lax.axis_size("seg")
    first_point = device_index * n_own
    n_points = device_count * n_own
    forward = [(i, i + 1) for i in range(device_count - 1)]
    backward = [(b, a) for a, b in forward]
    rows = TILE_ROWS
    n_chunks = n_rows // rows

    first = lax.ppermute(points[:1], "seg", backward)
    lows, highs = [], []
    for c in range(n_chunks):
        at = slice(c * rows, (c + 1) * rows)
        lows.append(lax.ppermute(points[n_own - 3 :, at], "seg", forward))
        highs.append(lax.ppermute(points[1:3, at], "seg", backward))

    step = points[1:].astype(jnp.float32) - points[:-1].astype(jnp.float32)
    inner = jnp.sum(step * step, axis=(1, 2))
    step = first[0].astype(jnp.float32) - points[n_own - 1].astype(jnp.float32)
    edge = jnp.sum(step * step)
    partial = jnp.concatenate([inner, edge[None]])
    own_squares = lax.psum(partial, "par")
    squares = lax.all_gather(own_squares, "seg", axis=0, tiled=True)
    index = jnp.arange(n_points, dtype=jnp.int32)
    lengths = jnp.where(index < n_points - 1, jnp.sqrt(squares), 0.0)
    ends = jnp.cumsum(lengths)
    arcs = jnp.concatenate([jnp.zeros((1,), jnp.float32), ends[:-1]])
    total = arcs[n_points - 1]
    target = total * (
        source_segment.astype(jnp.float32) + numerators.astype(jnp.float32) / 65536.0
    ) / (n_points - 1)
    fractions = (target - arcs[source_segment]) / lengths[source_segment]
    arc = lax.dynamic_slice(arcs, (first_point,), (n_own,)) / total
    buffer_rows = source_segment - first_point + LOW

    out = None
    for c in range(n_chunks):
        out = place(
            c, rows, buffer_rows, fractions, points, first, lows[c], highs[c], out
        )
    return (out, arc)


def solution(mesh):
    return jax.shard_map(
        per_device,
        mesh=mesh,
        in_specs=(P("seg", "par", None), P("seg"), P("seg")),
        out_specs=(P("seg", "par", None), P("seg")),
        check_vma=False,
    )
```

time: 236 us -> 159 us (0.67)
  waiting for transfers between devices: 130 us -> 13.1 us
  blocking collectives: 25.6 us -> 74.7 us
  local copies, waits for them, and re-layouts: 43.9 us -> 12.4 us
  starting transfers between devices: 7.77 us -> 27.6 us
  Pallas kernels: 0 us -> 15.4 us
  other arithmetic: 27.1 us -> 13.8 us
    ppermute x2 -> x9, waiting for transfers between devices: 130 us -> 13.1 us  [the longest x4 13.1 us: per_device(): lows.append(lax.ppermute(points[n_own - 3:, at], 'seg', forward))]
    unnamed x1, blocking collectives: 19.8 us -> 68.7 us
    gather x4 -> x2, local copies, waits for them, and re-layouts: 21.2 us -> 1.29 us  [per_device(): fractions = (target - arcs[source_segment]) / lengths[source_segment]]
    ppermute x2 -> x9, starting transfers between devices: 7.77 us -> 27.6 us  [the longest x4 21.1 us: per_device(): lows.append(lax.ppermute(points[n_own - 3:, at], 'seg', forward))]
    pallas_call x0 -> x4, Pallas kernels: none -> 15.4 us  [place(): pl.pallas_call(functools.partial(place_kernel, chunk, n_own, rows, prev i...]
    unnamed x9 -> x17, local copies, waits for them, and re-layouts: 14 us -> 2.6 us
    convert_element_type x1 -> x0, other arithmetic: 10.2 us -> none  [per_device(): (start_rows + fraction[:, None, None] * (end_rows - start_rows)).astype(j...]
    reduce_sum x3 -> x2, other arithmetic: 13.3 us -> 10.2 us  [the longest x1 7.78 us: per_device(): inner = jnp.sum(step * step, axis=(1, 2))]
  transfers between devices with their start and end apart: 2 -> 9, of which waited for: 1 -> 1; matrix products, arithmetic and copies ran while one was open for 6% -> 15% of each run, Pallas kernels for 0% -> 7%
where the time goes in v1:
time: 159 us; the launch traced here: 158 us
  blocking collectives  74.7 us (47%)
  starting transfers between devices  27.6 us (17%)
  Pallas kernels  15.4 us (10%)
  other arithmetic  13.8 us (9%)
  waiting for transfers between devices  13.1 us (8%)
  local copies, waits for them, and re-layouts  12.4 us (8%)
    unnamed x1, blocking collectives  68.7 us
    ppermute x4, starting transfers between devices, per_device(): lows.append(lax.ppermute(points[n_own - 3:, at], 'seg', forward))  21.1 us
    pallas_call x4, Pallas kernels, place(): pl.pallas_call(functools.partial(place_kernel, chunk, n_own, rows, prev i...  15.4 us
    ppermute x4, waiting for transfers between devices, per_device(): lows.append(lax.ppermute(points[n_own - 3:, at], 'seg', forward))  13.1 us
    reduce_sum x1, other arithmetic, per_device(): inner = jnp.sum(step * step, axis=(1, 2))  7.78 us
    psum x1, blocking collectives, per_device(): own_squares = lax.psum(partial, 'par')  5.96 us
    ppermute x4, starting transfers between devices, per_device(): highs.append(lax.ppermute(points[1:3, at], 'seg', backward))  5.15 us
    slice x1, local copies, waits for them, and re-layouts, per_device(): lows.append(lax.ppermute(points[n_own - 3:, at], 'seg', forward))  3.59 us
  transfers between devices with their start and end apart: 9, of which 1 were waited for; matrix products, arithmetic and copies ran while one was open for 15% of the time, Pallas kernels for 7%

profile of v1, /device:TPU:0, one launch (start us, length us, event | category | flops | bytes accessed | tf_op | source)
XLA Modules:
  0.0 158.3 jit_solution(12117169023168283810)
XLA Ops:
  0.6 1.3 slice.49
  1.9 1.3 collective-permute-start
  3.2 3.0 %fusion.1 = (bf16[2,8,16384]{2,1,0:T(8,128)(2,1)}, bf16[2,8,16384]{2,1,0:T(8,128)(2,1)}, bf16[2,8,16384]{2,1,0:T(8,128)(2,1)}, bf16[2,8,16384]{2,1,0:T(8,128)(2,1)}) fusion(bf16[8,32,16384]{2,1,0:T(8,128)(2,1)} %points.7), kind=kLoop, calls=%fused_computation.14 | loop fusion | bytes 4194304 | tf_op jit(solution)/shard_map/slice | solution.py:110
  6.2 1.3 collective-permute-start.8
  7.5 1.3 collective-permute-start.6
  8.8 3.6 %fusion.2 = (bf16[3,8,16384]{2,1,0:T(8,128)(2,1)}, bf16[3,8,16384]{2,1,0:T(8,128)(2,1)}, bf16[3,8,16384]{2,1,0:T(8,128)(2,1)}, bf16[3,8,16384]{2,1,0:T(8,128)(2,1)}) fusion(bf16[8,32,16384]{2,1,0:T(8,128)(2,1)} %points.7), kind=kLoop, calls=%fused_computation.15 | loop fusion | bytes 6291456 | tf_op jit(solution)/shard_map/slice | solution.py:109
  12.4 7.8 %collective-permute-start.7 = (bf16[3,8,16384]{2,1,0:T(8,128)(2,1)}, bf16[3,8,16384]{2,1,0:T(8,128)(2,1)}, u32[]{:S(2)}, u32[]{:S(2)}) collective-permute-start(bf16[3,8,16384]{2,1,0:T(8,128)(2,1)} %get-tuple-element.6), channel_id=1, source_target_pairs={{0,4},{4,8},{8,12},{12,16},{16,20},{20,24},{24,28},{1,5},{5,9},{9,... | collective-permute-start | bytes 2359304 | tf_op jit(solution)/shard_map/ppermute | solution.py:109
  20.1 4.0 %collective-permute-start.5 = (bf16[3,8,16384]{2,1,0:T(8,128)(2,1)}, bf16[3,8,16384]{2,1,0:T(8,128)(2,1)S(1)}, u32[]{:S(2)}, u32[]{:S(2)}) collective-permute-start(bf16[3,8,16384]{2,1,0:T(8,128)(2,1)} %get-tuple-element.7), channel_id=1, source_target_pairs={{0,4},{4,8},{8,12},{12,16},{16,20},{20,24},{24,28},{1,5},{5,9},{9,... | collective-permute-start | bytes 2359304 | tf_op jit(solution)/shard_map/ppermute | solution.py:109
  24.1 7.8 %multiply_reduce_fusion = f32[7]{0:T(128)S(1)} fusion(bf16[8,32,16384]{2,1,0:T(8,128)(2,1)} %points.7), kind=kLoop, calls=%fused_computation.2 | loop fusion | flops 18350072 | bytes 14680092 | tf_op jit(solution)/shard_map/reduce_sum | solution.py:113
  31.9 0.5 compare_select_fusion
  32.4 0.6 dynamic-slice
  33.0 3.9 %collective-permute-start.3 = (bf16[3,8,16384]{2,1,0:T(8,128)(2,1)}, bf16[3,8,16384]{2,1,0:T(8,128)(2,1)S(1)}, u32[]{:S(2)}, u32[]{:S(2)}) collective-permute-start(bf16[3,8,16384]{2,1,0:T(8,128)(2,1)} %get-tuple-element.8), channel_id=1, source_target_pairs={{0,4},{4,8},{8,12},{12,16},{16,20},{20,24},{24,28},{1,5},{5,9},{9,... | collective-permute-start | bytes 2359304 | tf_op jit(solution)/shard_map/ppermute | solution.py:109
  37.0 2.4 %multiply_reduce_fusion.1 = f32[]{:T(128)} fusion(bf16[1,32,16384]{2,1,0:T(8,128)(2,1)S(1)} %collective-permute-done.first, bf16[8,32,16384]{2,1,0:T(8,128)(2,1)} %points.7), kind=kLoop, calls=%fused_computation.3 | loop fusion | flops 2621439 | bytes 2097156 | tf_op jit(solution)/shard_map/reduce_sum | solution.py:115
  39.3 0.7 pad_maximum_fusion
  40.6 6.0 %psum.7 = f32[8]{0:T(128)S(1)} all-reduce(f32[8]{0:T(128)S(1)} %pad_maximum_fusion), channel_id=1, replica_groups=mesh['seg'=8,'par'=4] {'par'}, use_global_device_ids=true, to_apply=%region_2.0 | all-reduce | flops 8 | bytes 64 | tf_op jit(solution)/shard_map/psum | solution.py:117
  46.6 0.2 dynamic-update-slice
  46.8 68.7 %all-reduce = f32[64]{0:T(128)S(1)} all-reduce(f32[64]{0:T(128)S(1)} %dynamic-update-slice), channel_id=1, replica_groups=mesh['seg'=8,'par'=4] {'seg'}, use_global_device_ids=true, to_apply=%add | all-reduce | flops 64 | bytes 512
  115.6 1.3 collective-permute-start.4
  116.9 5.4 %collective-permute-start.1 = (bf16[3,8,16384]{2,1,0:T(8,128)(2,1)}, bf16[3,8,16384]{2,1,0:T(8,128)(2,1)}, u32[]{:S(2)}, u32[]{:S(2)}) collective-permute-start(bf16[3,8,16384]{2,1,0:T(8,128)(2,1)} %get-tuple-element.9), channel_id=1, source_target_pairs={{0,4},{4,8},{8,12},{12,16},{16,20},{20,24},{24,28},{1,5},{5,9},{9,... | collective-permute-start | bytes 2359304 | tf_op jit(solution)/shard_map/ppermute | solution.py:109
  122.5 0.5 slice.66
  123.0 0.6 gather_fusion.1
  123.7 1.3 collective-permute-start.2
  125.2 0.7 gather_fusion
  125.8 1.1 subtract_divide_fusion.fractions
  126.9 3.9 %shard_map.50.rest_0_ = bf16[8,32,16384]{2,1,0:T(8,128)(2,1)} custom-call(s32[8]{0:T(128)} %get-tuple-element.13.buffer_rows, f32[8]{0:T(128)} %subtract_divide_fusion.fractions, bf16[8,32,16384]{2,1,0:T(8,128)(2,1)} %points.7, bf16[1,32,16384]{2,1,0:T(8,128)(2,1)} %copy-done, bf16[3,8,16384]{2,1,0:T(8,128)(2,1)} %collective-permute-done.7.low, ...), custom_call_target="tpu_custom_call" | custom-call | flops 4194304 | bytes 5767168 | tf_op jit(solution)/shard_map/pallas_call | solution.py:76
  130.8 0.9 copy-done.1
  131.7 3.9 %shard_map.51.rest_0_ = bf16[8,32,16384]{2,1,0:T(8,128)(2,1)} custom-call(s32[8]{0:T(128)} %get-tuple-element.13.buffer_rows, f32[8]{0:T(128)} %subtract_divide_fusion.fractions, bf16[8,32,16384]{2,1,0:T(8,128)(2,1)} %points.7, bf16[1,32,16384]{2,1,0:T(8,128)(2,1)} %copy-done, bf16[3,8,16384]{2,1,0:T(8,128)(2,1)} %copy-done.1, ...), custom_call_target="tpu_custom_call", output_to_operand_aliasing={{}: (6, {})} | custom-call | flops 4194304 | bytes 5767168 | tf_op jit(solution)/shard_map/pallas_call | solution.py:76
  135.6 0.9 copy-done.2
  136.4 3.9 %shard_map.52.rest_0_ = bf16[8,32,16384]{2,1,0:T(8,128)(2,1)} custom-call(s32[8]{0:T(128)} %get-tuple-element.13.buffer_rows, f32[8]{0:T(128)} %subtract_divide_fusion.fractions, bf16[8,32,16384]{2,1,0:T(8,128)(2,1)} %points.7, bf16[1,32,16384]{2,1,0:T(8,128)(2,1)} %copy-done, bf16[3,8,16384]{2,1,0:T(8,128)(2,1)} %copy-done.2, ...), custom_call_target="tpu_custom_call", output_to_operand_aliasing={{}: (6, {})} | custom-call | flops 4194304 | bytes 5767168 | tf_op jit(solution)/shard_map/pallas_call | solution.py:76
  140.3 1.1 dynamic-slice_divide_fusion
  141.4 13.1 %collective-permute-done.1.low = bf16[3,8,16384]{2,1,0:T(8,128)(2,1)} collective-permute-done((bf16[3,8,16384]{2,1,0:T(8,128)(2,1)}, bf16[3,8,16384]{2,1,0:T(8,128)(2,1)}, u32[]{:S(2)}, u32[]{:S(2)}) %collective-permute-start.1) | collective-permute-done | bytes 786464 | tf_op jit(solution)/shard_map/ppermute | solution.py:109
  154.5 3.9 %shard_map.53 = bf16[8,32,16384]{2,1,0:T(8,128)(2,1)} custom-call(s32[8]{0:T(128)} %get-tuple-element.13.buffer_rows, f32[8]{0:T(128)} %subtract_divide_fusion.fractions, bf16[8,32,16384]{2,1,0:T(8,128)(2,1)} %points.7, bf16[1,32,16384]{2,1,0:T(8,128)(2,1)} %copy-done, ...), custom_call_target="tpu_custom_call", output_to_operand_aliasing={{}: (6, {})} | custom-call | flops 4194304 | bytes 5767168 | tf_op jit(solution)/shard_map/pallas_call | solution.py:76
  (27 shorter events, 0.4 us)
Async XLA Ops:
  1.9 31.1 %collective-permute-start = (bf16[1,32,16384]{2,1,0:T(8,128)(2,1)S(1)}, bf16[1,32,16384]{2,1,0:T(8,128)(2,1)S(1)}, u32[]{:S(2)}, u32[]{:S(2)}) collective-permute-start(bf16[1,32,16384]{2,1,0:T(8,128)(2,1)S(1)} %slice.49), channel_id=1, source_target_pairs={{4,0},{8,4},{12,8},{16,12},{20,16},{24,20},{28,24},{5,1},{9,5},{13... | collective-permute-start | bytes 3145736 | tf_op jit(solution)/shard_map/ppermute | solution.py:105
  6.2 109.4 %collective-permute-start.8 = (bf16[2,8,16384]{2,1,0:T(8,128)(2,1)}, bf16[2,8,16384]{2,1,0:T(8,128)(2,1)}, u32[]{:S(2)}, u32[]{:S(2)}) collective-permute-start(bf16[2,8,16384]{2,1,0:T(8,128)(2,1)} %get-tuple-element.2), channel_id=1, source_target_pairs={{4,0},{8,4},{12,8},{16,12},{20,16},{24,20},{28,24},{5,1},{9,5},{13... | collective-permute-start | bytes 1572872 | tf_op jit(solution)/shard_map/ppermute | solution.py:110
  7.5 109.4 %collective-permute-start.6 = (bf16[2,8,16384]{2,1,0:T(8,128)(2,1)}, bf16[2,8,16384]{2,1,0:T(8,128)(2,1)S(1)}, u32[]{:S(2)}, u32[]{:S(2)}) collective-permute-start(bf16[2,8,16384]{2,1,0:T(8,128)(2,1)} %get-tuple-element.3), channel_id=1, source_target_pairs={{4,0},{8,4},{12,8},{16,12},{20,16},{24,20},{28,24},{5,1},{9,5},{13... | collective-permute-start | bytes 1572872 | tf_op jit(solution)/shard_map/ppermute | solution.py:110
  12.4 19.6 %copy-start.4 = (s32[8]{0:T(128)S(1)}, s32[8]{0:T(128)}, u32[]{:S(2)}) copy-start(s32[8]{0:T(128)} %param.4) | copy-start | bytes 100
  12.4 20.1 %copy-start.6 = (u32[32]{0:T(128)S(1)}, u32[32]{0:T(128)}, u32[]{:S(2)}) copy-start(u32[32]{0:T(128)} %constant.33) | copy-start | bytes 388
  12.4 111.3 %collective-permute-start.7 = (bf16[3,8,16384]{2,1,0:T(8,128)(2,1)}, bf16[3,8,16384]{2,1,0:T(8,128)(2,1)}, u32[]{:S(2)}, u32[]{:S(2)}) collective-permute-start(bf16[3,8,16384]{2,1,0:T(8,128)(2,1)} %get-tuple-element.6), channel_id=1, source_target_pairs={{0,4},{4,8},{8,12},{12,16},{16,20},{20,24},{24,28},{1,5},{5,9},{9,... | collective-permute-start | bytes 2359304 | tf_op jit(solution)/shard_map/ppermute | solution.py:109
  20.1 110.6 %collective-permute-start.5 = (bf16[3,8,16384]{2,1,0:T(8,128)(2,1)}, bf16[3,8,16384]{2,1,0:T(8,128)(2,1)S(1)}, u32[]{:S(2)}, u32[]{:S(2)}) collective-permute-start(bf16[3,8,16384]{2,1,0:T(8,128)(2,1)} %get-tuple-element.7), channel_id=1, source_target_pairs={{0,4},{4,8},{8,12},{12,16},{16,20},{20,24},{24,28},{1,5},{5,9},{9,... | collective-permute-start | bytes 2359304 | tf_op jit(solution)/shard_map/ppermute | solution.py:109
  24.1 101.7 %copy-start.5 = (s32[8]{0:T(128)S(1)}, s32[8]{0:T(128)}, u32[]{:S(2)}) copy-start(s32[8]{0:T(128)} %param.5) | copy-start | bytes 100
  33.0 93.9 %copy-start = (bf16[1,32,16384]{2,1,0:T(8,128)(2,1)}, bf16[1,32,16384]{2,1,0:T(8,128)(2,1)S(1)}, u32[]{:S(2)}) copy-start(bf16[1,32,16384]{2,1,0:T(8,128)(2,1)S(1)} %collective-permute-done.first) | copy-start | bytes 3145732
  33.0 102.5 %collective-permute-start.3 = (bf16[3,8,16384]{2,1,0:T(8,128)(2,1)}, bf16[3,8,16384]{2,1,0:T(8,128)(2,1)S(1)}, u32[]{:S(2)}, u32[]{:S(2)}) collective-permute-start(bf16[3,8,16384]{2,1,0:T(8,128)(2,1)} %get-tuple-element.8), channel_id=1, source_target_pairs={{0,4},{4,8},{8,12},{12,16},{16,20},{20,24},{24,28},{1,5},{5,9},{9,... | collective-permute-start | bytes 2359304 | tf_op jit(solution)/shard_map/ppermute | solution.py:109
  115.6 19.9 %collective-permute-start.4 = (bf16[2,8,16384]{2,1,0:T(8,128)(2,1)}, bf16[2,8,16384]{2,1,0:T(8,128)(2,1)}, u32[]{:S(2)}, u32[]{:S(2)}) collective-permute-start(bf16[2,8,16384]{2,1,0:T(8,128)(2,1)} %get-tuple-element.4), channel_id=1, source_target_pairs={{4,0},{8,4},{12,8},{16,12},{20,16},{24,20},{28,24},{5,1},{9,5},{13... | collective-permute-start | bytes 1572872 | tf_op jit(solution)/shard_map/ppermute | solution.py:110
  116.9 13.9 %copy-start.3 = (bf16[2,8,16384]{2,1,0:T(8,128)(2,1)}, bf16[2,8,16384]{2,1,0:T(8,128)(2,1)S(1)}, u32[]{:S(2)}) copy-start(bf16[2,8,16384]{2,1,0:T(8,128)(2,1)S(1)} %collective-permute-done.6.high) | copy-start | bytes 1572868
  116.9 37.6 %collective-permute-start.1 = (bf16[3,8,16384]{2,1,0:T(8,128)(2,1)}, bf16[3,8,16384]{2,1,0:T(8,128)(2,1)}, u32[]{:S(2)}, u32[]{:S(2)}) collective-permute-start(bf16[3,8,16384]{2,1,0:T(8,128)(2,1)} %get-tuple-element.9), channel_id=1, source_target_pairs={{0,4},{4,8},{8,12},{12,16},{16,20},{20,24},{24,28},{1,5},{5,9},{9,... | collective-permute-start | bytes 2359304 | tf_op jit(solution)/shard_map/ppermute | solution.py:109
  123.7 17.8 %collective-permute-start.2 = (bf16[2,8,16384]{2,1,0:T(8,128)(2,1)}, bf16[2,8,16384]{2,1,0:T(8,128)(2,1)}, u32[]{:S(2)}, u32[]{:S(2)}) collective-permute-start(bf16[2,8,16384]{2,1,0:T(8,128)(2,1)} %get-tuple-element.5), channel_id=1, source_target_pairs={{4,0},{8,4},{12,8},{16,12},{20,16},{24,20},{28,24},{5,1},{9,5},{13... | collective-permute-start | bytes 1572872 | tf_op jit(solution)/shard_map/ppermute | solution.py:110
  130.8 0.9 copy-start.1
  135.6 0.9 copy-start.2

commit v2 on v1

v2 whole, which is shorter than its diff:
```python
import functools

import jax
import jax.numpy as jnp
import numpy as np
from jax import lax
from jax.experimental import pallas as pl
from jax.experimental.pallas import tpu as pltpu
from jax.sharding import PartitionSpec as P


TILE_ROWS = 8
COL_BLOCKS = 4
LOW = 3
HIGH = 3
ROW, EDGE_ROW, AT_LOCAL, AT_EDGE, AT_FAR, RELAYED = range(6)


def place_kernel(
    rows, relays, has_prev,
    table, buffer_rows, fractions, points, edge, local, *rest
):
    fars, rest = rest[:relays], rest[relays:]
    if has_prev:
        rest = rest[1:]
    out, buf, res, in_sem, out_sem = rest
    n_own, _, width = points.shape
    cols = width // COL_BLOCKS
    row = pl.multiple_of(table[ROW], rows)
    edge_row = pl.multiple_of(table[EDGE_ROW], rows)

    def in_copy(c, k, far):
        at = pl.ds(c * cols, cols)
        src, start, count = (
            (points.at[:, pl.ds(row, rows), at], LOW, n_own),
            (edge.at[:, pl.ds(edge_row, rows), at], table[AT_EDGE], 1),
            (local.at[:, :, at], table[AT_LOCAL], local.shape[0]),
            (far.at[:, :, at], table[AT_FAR], far.shape[0]),
        )[k]
        dst = buf.at[pl.ds(start, count), :, at]
        return pltpu.make_async_copy(src, dst, in_sem.at[c, k])

    def out_copy(c):
        at = pl.ds(c * cols, cols)
        return pltpu.make_async_copy(
            res.at[:, :, at], out.at[:, pl.ds(row, rows), at], out_sem.at[c]
        )

    for c in range(COL_BLOCKS):
        for k in range(3):
            in_copy(c, k, fars[0]).start()
        if len(fars) == 1:
            in_copy(c, 3, fars[0]).start()
        else:

            @pl.when(table[RELAYED] == 1)
            def _():
                in_copy(c, 3, fars[1]).start()

            @pl.when(table[RELAYED] == 0)
            def _():
                in_copy(c, 3, fars[0]).start()

    for c in range(COL_BLOCKS):
        for k in range(4):
            in_copy(c, k, fars[0]).wait()
        at = pl.ds(c * cols, cols)

        @pl.loop(0, n_own)
        def _(j):
            start = buf[buffer_rows[j], :, at].astype(jnp.float32)
            end = buf[buffer_rows[j] + 1, :, at].astype(jnp.float32)
            res[j, :, at] = (start + fractions[j] * (end - start)).astype(res.dtype)

        out_copy(c).start()
    for c in range(COL_BLOCKS):
        out_copy(c).wait()


def place(rows, table, buffer_rows, fractions, points, edge, local, fars, prev):
    n_own, _, width = points.shape
    held = LOW + n_own + HIGH
    hbm = pl.BlockSpec(memory_space=pl.ANY)
    smem = pl.BlockSpec(memory_space=pltpu.SMEM)
    args = [table, buffer_rows, fractions, points, edge, local, *fars]
    if prev is not None:
        args.append(prev)
    moved = (held + n_own) * rows * width * points.dtype.itemsize
    return pl.pallas_call(
        functools.partial(place_kernel, rows, len(fars), prev is not None),
        out_shape=jax.ShapeDtypeStruct(points.shape, points.dtype),
        in_specs=[smem] * 3 + [hbm] * (len(args) - 3),
        out_specs=hbm,
        scratch_shapes=[
            pltpu.VMEM((held, rows, width), points.dtype),
            pltpu.VMEM((n_own, rows, width), points.dtype),
            pltpu.SemaphoreType.DMA((COL_BLOCKS, 4)),
            pltpu.SemaphoreType.DMA((COL_BLOCKS,)),
        ],
        input_output_aliases={} if prev is None else {len(args) - 1: 0},
        cost_estimate=pl.CostEstimate(
            flops=4 * n_own * rows * width, bytes_accessed=moved, transcendentals=0
        ),
    )(*args)


def squares(start, end):
    step = end.astype(jnp.float32) - start.astype(jnp.float32)
    return jnp.sum(step * step, axis=(1, 2))


def finish(all_squares, first_point, n_own, n_points, source_segment, numerators):
    index = jnp.arange(n_points, dtype=jnp.int32)
    lengths = jnp.where(index < n_points - 1, jnp.sqrt(all_squares), 0.0)
    arcs = jnp.concatenate([jnp.zeros((1,), jnp.float32), jnp.cumsum(lengths)[:-1]])
    total = arcs[n_points - 1]
    target = total * (
        source_segment.astype(jnp.float32) + numerators.astype(jnp.float32) / 65536.0
    ) / (n_points - 1)
    fractions = (target - arcs[source_segment]) / lengths[source_segment]
    arc = lax.dynamic_slice(arcs, (first_point,), (n_own,)) / total
    return fractions, arc


def chain_device(points, source_segment, numerators):
    n_own, n_rows, _ = points.shape
    device_index = lax.axis_index("seg")
    device_count = lax.axis_size("seg")
    first_point = device_index * n_own
    n_points = device_count * n_own
    forward = [(i, i + 1) for i in range(device_count - 1)]
    backward = [(b, a) for a, b in forward]
    rows = TILE_ROWS
    n_chunks = n_rows // rows

    first = lax.ppermute(points[:1], "seg", backward)
    lows, highs = [], []
    for c in range(n_chunks):
        at = slice(c * rows, (c + 1) * rows)
        lows.append(lax.ppermute(points[n_own - LOW :, at], "seg", forward))
        highs.append(lax.ppermute(points[1:HIGH, at], "seg", backward))
    inner = squares(points[:-1], points[1:])
    edge = squares(points[n_own - 1 :], first)
    own_squares = lax.psum(jnp.concatenate([inner, edge]), "par")
    all_squares = lax.all_gather(own_squares, "seg", axis=0, tiled=True)
    fractions, arc = finish(
        all_squares, first_point, n_own, n_points, source_segment, numerators
    )
    buffer_rows = source_segment - first_point + LOW
    out = None
    for c in range(n_chunks):
        table = jnp.array(
            [c * rows, c * rows, 0, LOW + n_own, LOW + n_own + 1, 0], jnp.int32
        )
        out = place(
            rows, table, buffer_rows, fractions, points, first,
            lows[c], (highs[c],), out,
        )
    return (out, arc)


def paired_device(points, source_segment, numerators):
    n_own, n_rows, width = points.shape
    device_index = lax.axis_index("seg")
    count = lax.axis_size("seg")
    pairs = count // 2
    side = device_index % 2
    even = side == 0
    first_point = device_index * n_own
    n_points = count * n_own
    rows = TILE_ROWS
    steps = n_rows // rows
    half = n_rows // 2

    local_pairs = [(2 * k, 2 * k + 1) for k in range(pairs)]
    local_pairs += [(b, a) for a, b in local_pairs]
    far_pairs = [(2 * k + 1, 2 * k + 2) for k in range(pairs - 1)]
    far_pairs += [(b, a) for a, b in far_pairs]

    def relayed(source, step):
        k = source // 2
        return (k if source % 2 == 0 else pairs - 1 - k) * steps > step * pairs

    relay_of = lambda source: source + 1 if source % 2 == 0 else source - 1
    hop1 = [[(a, relay_of(a)) for a, b in far_pairs if relayed(a, s)] for s in range(steps)]
    hop2 = [[(relay_of(a), b) for a, b in far_pairs if relayed(a, s)] for s in range(steps)]
    direct = [[(a, b) for a, b in far_pairs if not relayed(a, s)] for s in range(steps)]

    def border(to_next):
        start = jnp.where(to_next, n_own - 1, 0), jnp.where(to_next, half, 0), 0
        return lax.dynamic_slice(points, start, (1, half, width))

    def row_of(is_even, step):
        return jnp.where(is_even, step, steps - 1 - step) * rows

    edge_far = lax.ppermute(border(~even), "seg", far_pairs)
    edge_local = lax.ppermute(border(even), "seg", local_pairs)

    far_payload, local_payload = [], []
    for s in range(steps):
        n_far = 3 if s < steps // 2 else 2
        n_local = 5 - n_far
        far_start = jnp.where(even, 3 - n_far, n_own - 3)
        far_payload.append(
            lax.dynamic_slice(
                points, (far_start, row_of(~even, s), 0), (n_far, rows, width)
            )
        )
        local_start = jnp.where(even, n_own - 3, 3 - n_local)
        local_payload.append(
            lax.dynamic_slice(
                points, (local_start, row_of(~even, s), 0), (n_local, rows, width)
            )
        )
    middle, relay, far, local = {}, {}, {}, {}
    for s in range(steps):
        if hop1[s]:
            middle[s] = lax.ppermute(far_payload[s], "seg", hop1[s])
        local[s] = lax.ppermute(local_payload[s], "seg", local_pairs)
    for s in range(steps):
        if direct[s]:
            far[s] = lax.ppermute(far_payload[s], "seg", direct[s])
        if hop2[s]:
            relay[s] = lax.ppermute(middle[s], "seg", hop2[s])

    from_prev = jnp.where(even, edge_far, edge_local)
    from_next = jnp.where(even, edge_local, edge_far)
    partial = jnp.concatenate(
        [
            squares(from_prev, points[:1, half:]),
            squares(points[:-1], points[1:]),
            squares(points[n_own - 1 :, :half], from_next),
        ]
    )
    partial = lax.psum(partial, "par")
    spread = lax.dynamic_update_slice(
        jnp.zeros((n_points + 1,), jnp.float32), partial, (first_point,)
    )
    shift = 1
    while shift < pairs:
        ring = [(2 * k, 2 * ((k - shift) % pairs)) for k in range(pairs)]
        ring += [(2 * k + 1, 2 * ((k + shift) % pairs) + 1) for k in range(pairs)]
        spread = spread + lax.ppermute(spread, "seg", ring)
        shift *= 2
    cross = [(2 * k, 2 * ((k - 1) % pairs) + 1) for k in range(pairs)]
    cross += [(2 * k + 1, 2 * ((k + 1) % pairs)) for k in range(pairs)]
    spread = spread + lax.ppermute(spread, "seg", cross)
    fractions, arc = finish(
        spread[1:], first_point, n_own, n_points, source_segment, numerators
    )
    buffer_rows = source_segment - first_point + LOW

    target_relayed = np.zeros((steps, count), np.int32)
    for s in range(steps):
        for _, b in hop2[s]:
            target_relayed[s, b] = 1
    out = None
    for s in range(steps):
        row = row_of(even, s)
        if s < steps // 2:
            at_local = jnp.where(even, LOW + n_own + 1, 0)
            at_edge = jnp.where(even, LOW + n_own, LOW - 1)
            at_far = jnp.where(even, 0, LOW + n_own)
            edge = edge_local
        else:
            at_local = jnp.where(even, LOW + n_own, 0)
            at_edge = jnp.where(even, LOW - 1, LOW + n_own)
            at_far = jnp.where(even, 0, LOW + n_own + 1)
            edge = edge_far
        flag = jnp.asarray(target_relayed[s])[device_index]
        table = jnp.stack(
            [row, row % half, at_local, at_edge, at_far, flag]
        ).astype(jnp.int32)
        fars = tuple(d[s] for d in (far, relay) if s in d)
        out = place(
            rows, table, buffer_rows, fractions, points, edge,
            local[s], fars, out,
        )
    return (out, arc)


def is_paired(mesh):
    names = mesh.axis_names
    devices = np.moveaxis(mesh.devices, names.index("seg"), 0)
    devices = devices.reshape(devices.shape[0], -1)[:, 0]
    count = len(devices)
    pairs = count // 2
    if count % 2 or pairs < 2 or pairs & (pairs - 1):
        return False
    places = [getattr(device, "coords", None) for device in devices]
    if any(place is None for place in places):
        return False
    return all(
        (place[0], place[2]) == (i % 2, i // 2) and place[1] == places[0][1]
        for i, place in enumerate(places)
    )


def solution(mesh):
    paired = is_paired(mesh)

    def body(*args):
        return (paired_device if paired else chain_device)(*args)

    return jax.shard_map(
        body,
        mesh=mesh,
        in_specs=(P("seg", "par", None), P("seg"), P("seg")),
        out_specs=(P("seg", "par", None), P("seg")),
        check_vma=False,
    )
```

time: 159 us -> 160 us (level)
  blocking collectives: 74.7 us -> 6.19 us
  waiting for transfers between devices: 13.1 us -> 56.4 us
  starting transfers between devices: 27.6 us -> 48.4 us
  local copies, waits for them, and re-layouts: 12.4 us -> 16.8 us
    unnamed x1 -> x0, blocking collectives: 68.7 us -> none
    ppermute x9 -> x18, waiting for transfers between devices: 13.1 us -> 56.4 us  [the longest x4 14.9 us: paired_device(): local[s] = lax.ppermute(local_payload[s], 'seg', local_pairs)]
    ppermute x9 -> x18, starting transfers between devices: 27.6 us -> 48.4 us  [the longest x3 10.3 us: paired_device(): relay[s] = lax.ppermute(middle[s], 'seg', hop2[s])]
    dynamic_slice x0 -> x6, local copies, waits for them, and re-layouts: none -> 10.2 us  [the longest x1 3.33 us: paired_device(): lax.dynamic_slice(points, (far_start, row_of(~even, s), 0), (n_far, rows,...]
    slice x5 -> x2, local copies, waits for them, and re-layouts: 8.43 us -> 0.63 us  [the longest x1 0.52 us: finish(): total = arcs[n_points - 1]]
    another operation x0 -> x4, local copies, waits for them, and re-layouts: none -> 4.33 us  [paired_device(): jnp.stack([row, row % half, at_local, at_edge, at_far, flag])]
    unnamed x17 -> x20, local copies, waits for them, and re-layouts: 2.6 us -> 0.04 us
  transfers between devices with their start and end apart: 9 -> 18, of which waited for: 1 -> 9; matrix products, arithmetic and copies ran while one was open for 15% -> 18% of each run, Pallas kernels for 7% -> 7%
where the time goes in v2:
time: 160 us; the launch traced here: 159 us
  waiting for transfers between devices  56.4 us (35%)
  starting transfers between devices  48.4 us (30%)
  local copies, waits for them, and re-layouts  16.8 us (10%)
  Pallas kernels  15.5 us (10%)
  other arithmetic  14.8 us (9%)
  blocking collectives  6.19 us (4%)
    pallas_call x4, Pallas kernels, place(): pl.pallas_call(functools.partial(place_kernel, rows, len(fars), prev is n...  15.5 us
    ppermute x4, waiting for transfers between devices, paired_device(): local[s] = lax.ppermute(local_payload[s], 'seg', local_pairs)  14.9 us
    ppermute x1, waiting for transfers between devices, paired_device(): edge_local = lax.ppermute(border(even), 'seg', local_pairs)  12.1 us
    ppermute x3, waiting for transfers between devices, paired_device(): middle[s] = lax.ppermute(far_payload[s], 'seg', hop1[s])  11.2 us
    ppermute x3, starting transfers between devices, paired_device(): relay[s] = lax.ppermute(middle[s], 'seg', hop2[s])  10.3 us
    reduce_sum x2, other arithmetic, squares(): return jnp.sum(step * step, axis=(1, 2))  10.3 us
    ppermute x4, starting transfers between devices, paired_device(): local[s] = lax.ppermute(local_payload[s], 'seg', local_pairs)  10.2 us
    ppermute x1, starting transfers between devices, paired_device(): edge_local = lax.ppermute(border(even), 'seg', local_pairs)  9.92 us
  transfers between devices with their start and end apart: 18, of which 9 were waited for; matrix products, arithmetic and copies ran while one was open for 18% of the time, Pallas kernels for 7%

profile of v2, /device:TPU:0, one launch (start us, length us, event | category | flops | bytes accessed | tf_op | source)
XLA Modules:
  0.0 158.9 jit_solution(2941538705877676181)
XLA Ops:
  0.7 3.3 %constant_dynamic-slice_fusion.7 = (bf16[3,8,16384]{2,1,0:T(8,128)(2,1)S(1)}, bf16[3,8,16384]{2,1,0:T(8,128)(2,1)}, bf16[3,8,16384]{2,1,0:T(8,128)(2,1)}, bf16[3,8,16384]{2,1,0:T(8,128)(2,1)}) fusion(bf16[8,32,16384]{2,1,0:T(8,128)(2,1)} %points.7, s32[]{:T(128)S(6)} %select_n.190, s32[]{:T(128)S(6)} %select_n.192, s32[]{:T(128)S(6)} %select_n.189, ...), kind=kLoop, calls=%fused_computation.15 | loop fusion | bytes 6291480 | tf_op jit(solution)/shard_map/dynamic_slice | solution.py:205
  6.0 1.3 collective-permute-start.16
  7.3 2.3 %constant_dynamic-slice_fusion.8 = (bf16[1,16,16384]{2,1,0:T(8,128)(2,1)}, bf16[1,16,16384]{2,1,0:T(8,128)(2,1)}) fusion(bf16[8,32,16384]{2,1,0:T(8,128)(2,1)} %points.7, s32[]{:T(128)S(6)} %select_n.169, s32[]{:T(128)S(6)} %select_n.170, s32[]{:T(128)S(6)} %select_n.167, s32[]{:T(128)S(6)} %select_n.168), kind=kLoop, calls=%fused_computation.16 | loop fusion | bytes 2097168 | tf_op jit(solution)/shard_map/dynamic_slice | solution.py:191
  10.3 9.9 %collective-permute-start.1 = (bf16[1,16,16384]{2,1,0:T(8,128)(2,1)}, bf16[1,16,16384]{2,1,0:T(8,128)(2,1)S(1)}, u32[]{:S(2)}, u32[]{:S(2)}) collective-permute-start(bf16[1,16,16384]{2,1,0:T(8,128)(2,1)} %get-tuple-element.12), channel_id=1, source_target_pairs={{0,4},{8,12},{16,20},{24,28},{4,0},{12,8},{20,16},{28,24},{1,5},{9... | collective-permute-start | bytes 1572872 | tf_op jit(solution)/shard_map/ppermute | solution.py:197
  20.2 2.7 %constant_dynamic-slice_fusion = (bf16[2,8,16384]{2,1,0:T(8,128)(2,1)S(1)}, bf16[2,8,16384]{2,1,0:T(8,128)(2,1)}, bf16[2,8,16384]{2,1,0:T(8,128)(2,1)}, bf16[2,8,16384]{2,1,0:T(8,128)(2,1)}) fusion(bf16[8,32,16384]{2,1,0:T(8,128)(2,1)} %points.7, s32[]{:T(128)S(6)} %select_n.188, s32[]{:T(128)S(6)} %select_n.192, s32[]{:T(128)S(6)} %select_n.189, ...), kind=kLoop, calls=%fused_computation.8 | loop fusion | bytes 4194328 | tf_op jit(solution)/shard_map/dynamic_slice | solution.py:211
  22.9 7.8 %multiply_reduce_fusion = f32[7]{0:T(128)S(1)} fusion(bf16[8,32,16384]{2,1,0:T(8,128)(2,1)} %points.7), kind=kLoop, calls=%fused_computation.2 | loop fusion | flops 18350072 | bytes 14680092 | tf_op jit(solution)/shard_map/reduce_sum | solution.py:109
  32.6 10.2 %collective-permute-start.15 = (bf16[2,8,16384]{2,1,0:T(8,128)(2,1)S(1)}, bf16[2,8,16384]{2,1,0:T(8,128)(2,1)}, u32[]{:S(2)}, u32[]{:S(2)}) collective-permute-start(bf16[2,8,16384]{2,1,0:T(8,128)(2,1)S(1)} %get-tuple-element.8), channel_id=1, source_target_pairs={{0,4},{8,12},{16,20},{24,28},{4,0},{12,8},{20,16},{28,24},{1,5},{9... | collective-permute-start | bytes 1572872 | tf_op jit(solution)/shard_map/ppermute | solution.py:219
  42.8 12.1 %collective-permute-done.1.edge = bf16[1,16,16384]{2,1,0:T(8,128)(2,1)S(1)} collective-permute-done((bf16[1,16,16384]{2,1,0:T(8,128)(2,1)}, bf16[1,16,16384]{2,1,0:T(8,128)(2,1)S(1)}, u32[]{:S(2)}, u32[]{:S(2)}) %collective-permute-start.1) | collective-permute-done | bytes 524320 | tf_op jit(solution)/shard_map/ppermute | solution.py:197
  54.9 2.4 %multiply_reduce_fusion.2 = (f32[]{:T(128)}, f32[]{:T(128)}) fusion(bf16[1,16,16384]{2,1,0:T(8,128)(2,1)S(1)} %collective-permute-done.edge, bf16[1,16,16384]{2,1,0:T(8,128)(2,1)S(1)} %collective-permute-done.1.edge, bf16[8,32,16384]{2,1,0:T(8,128)(2,1)} %points.7, pred[]{:T(512)S(6)} %eq.10), kind=kLoop, calls=%fused_computation.4 | loop fusion | flops 3145726 | bytes 2097161 | tf_op jit(solution)/shard_map/reduce_sum | solution.py:109
  58.6 6.2 %psum.7 = f32[9]{0:T(128)S(1)} all-reduce(f32[9]{0:T(128)S(1)} %pad_maximum_fusion), channel_id=1, replica_groups=mesh['seg'=8,'par'=4] {'par'}, use_global_device_ids=true, to_apply=%region_3.4 | all-reduce | flops 9 | bytes 72 | tf_op jit(solution)/shard_map/psum | solution.py:235
  65.1 3.9 %collective-permute-start.2 = (f32[65]{0:T(128)S(1)}, f32[65]{0:T(128)S(1)}, u32[]{:S(2)}, u32[]{:S(2)}) collective-permute-start(f32[65]{0:T(128)S(1)} %dynamic_update_slice.5), channel_id=1, source_target_pairs={{0,24},{8,0},{16,8},{24,16},{4,12},{12,20},{20,28},{28,4},{1,25},{... | collective-permute-start | bytes 788 | tf_op jit(solution)/shard_map/ppermute | solution.py:243
  68.9 1.3 stack.77.table
  71.4 9.0 %collective-permute-done.2 = f32[65]{0:T(128)S(1)} collective-permute-done((f32[65]{0:T(128)S(1)}, f32[65]{0:T(128)S(1)}, u32[]{:S(2)}, u32[]{:S(2)}) %collective-permute-start.2) | collective-permute-done | bytes 292 | tf_op jit(solution)/shard_map/ppermute | solution.py:243
  80.6 2.4 %collective-permute-start.3 = (f32[65]{0:T(128)S(1)}, f32[65]{0:T(128)S(1)}, u32[]{:S(2)}, u32[]{:S(2)}) collective-permute-start(f32[65]{0:T(128)S(1)} %add_dynamic-update-slice_fusion), channel_id=1, source_target_pairs={{0,16},{8,24},{16,0},{24,8},{4,20},{12,28},{20,4},{28,12},{1,17},{... | collective-permute-start | bytes 788 | tf_op jit(solution)/shard_map/ppermute | solution.py:243
  83.0 1.3 stack.68.table
  85.0 3.4 %collective-permute-start.4 = (f32[65]{0:T(128)S(1)}, f32[65]{0:T(128)S(1)}, u32[]{:S(2)}, u32[]{:S(2)}) collective-permute-start(f32[65]{0:T(128)S(1)} %add.85), channel_id=1, source_target_pairs={{0,28},{8,4},{16,12},{24,20},{4,8},{12,16},{20,24},{28,0},{1,29},{... | collective-permute-start | bytes 788 | tf_op jit(solution)/shard_map/ppermute | solution.py:247
  89.1 2.2 %collective-permute-done.4 = f32[65]{0:T(128)S(1)} collective-permute-done((f32[65]{0:T(128)S(1)}, f32[65]{0:T(128)S(1)}, u32[]{:S(2)}, u32[]{:S(2)}) %collective-permute-start.4) | collective-permute-done | bytes 292 | tf_op jit(solution)/shard_map/ppermute | solution.py:247
  91.3 1.3 collective-permute-start.9
  92.6 2.4 %collective-permute-start.17 = (bf16[3,8,16384]{2,1,0:T(8,128)(2,1)}, bf16[3,8,16384]{2,1,0:T(8,128)(2,1)S(1)}, u32[]{:S(2)}, u32[]{:S(2)}) collective-permute-start(bf16[3,8,16384]{2,1,0:T(8,128)(2,1)} %collective-permute-done.16), channel_id=1, source_target_pairs={{0,8},{8,16},{16,24},{12,4},{20,12},{28,20},{1,9},{9,17},{17,25},{... | collective-permute-start | bytes 2359304 | tf_op jit(solution)/shard_map/ppermute | solution.py:224
  95.0 2.8 %collective-permute-start.14 = (bf16[3,8,16384]{2,1,0:T(8,128)(2,1)}, bf16[3,8,16384]{2,1,0:T(8,128)(2,1)S(1)}, u32[]{:S(2)}, u32[]{:S(2)}) collective-permute-start(bf16[3,8,16384]{2,1,0:T(8,128)(2,1)} %collective-permute-done.13), channel_id=1, source_target_pairs={{0,8},{8,16},{20,12},{28,20},{1,9},{9,17},{21,13},{29,21},{2,10},{... | collective-permute-start | bytes 2359304 | tf_op jit(solution)/shard_map/ppermute | solution.py:224
  99.2 4.9 %collective-permute-done.11.local = bf16[2,8,16384]{2,1,0:T(8,128)(2,1)} collective-permute-done((bf16[2,8,16384]{2,1,0:T(8,128)(2,1)}, bf16[2,8,16384]{2,1,0:T(8,128)(2,1)}, u32[]{:S(2)}, u32[]{:S(2)}) %collective-permute-start.11) | collective-permute-done | bytes 524320 | tf_op jit(solution)/shard_map/ppermute | solution.py:219
  104.1 11.2 %collective-permute-done.9 = bf16[2,8,16384]{2,1,0:T(8,128)(2,1)} collective-permute-done((bf16[2,8,16384]{2,1,0:T(8,128)(2,1)}, bf16[2,8,16384]{2,1,0:T(8,128)(2,1)}, u32[]{:S(2)}, u32[]{:S(2)}) %collective-permute-start.9) | collective-permute-done | bytes 524320 | tf_op jit(solution)/shard_map/ppermute | solution.py:218
  116.2 1.5 collective-permute-start.8
  117.7 1.5 collective-permute-start.6
  119.2 6.1 %collective-permute-done.14.rest_1_ = bf16[3,8,16384]{2,1,0:T(8,128)(2,1)S(1)} collective-permute-done((bf16[3,8,16384]{2,1,0:T(8,128)(2,1)}, bf16[3,8,16384]{2,1,0:T(8,128)(2,1)S(1)}, u32[]{:S(2)}, u32[]{:S(2)}) %collective-permute-start.14) | collective-permute-done | bytes 786464 | tf_op jit(solution)/shard_map/ppermute | solution.py:224
  125.3 5.1 %collective-permute-start.10 = (bf16[2,8,16384]{2,1,0:T(8,128)(2,1)}, bf16[2,8,16384]{2,1,0:T(8,128)(2,1)}, u32[]{:S(2)}, u32[]{:S(2)}) collective-permute-start(bf16[2,8,16384]{2,1,0:T(8,128)(2,1)} %collective-permute-done.9), channel_id=1, source_target_pairs={{0,8},{28,20},{1,9},{29,21},{2,10},{30,22},{3,11},{31,23}} | collective-permute-start | bytes 1572872 | tf_op jit(solution)/shard_map/ppermute | solution.py:224
  133.4 3.9 %shard_map.86.rest_2_ = bf16[8,32,16384]{2,1,0:T(8,128)(2,1)} custom-call(s32[6]{0:T(128)} %stack.77.table, s32[8]{0:T(128)} %get-tuple-element.15.buffer_rows, f32[8]{0:T(128)} %subtract_divide_fusion.fractions, bf16[8,32,16384]{2,1,0:T(8,128)(2,1)} %points.7, bf16[1,16,16384]{2,1,0:T(8,128)(2,1)} %copy-done.1, ...), custom_call_target="tpu_custom_call" | custom-call | flops 4194304 | bytes 5767168 | tf_op jit(solution)/shard_map/pallas_call | solution.py:89
  137.3 3.9 %shard_map.87.rest_2_ = bf16[8,32,16384]{2,1,0:T(8,128)(2,1)} custom-call(s32[6]{0:T(128)} %stack.74.table, s32[8]{0:T(128)} %get-tuple-element.15.buffer_rows, f32[8]{0:T(128)} %subtract_divide_fusion.fractions, bf16[8,32,16384]{2,1,0:T(8,128)(2,1)} %points.7, bf16[1,16,16384]{2,1,0:T(8,128)(2,1)} %copy-done.1, ...), custom_call_target="tpu_custom_call", output_to_operand_aliasing={{}: (8, {})} | custom-call | flops 4194304 | bytes 5767168 | tf_op jit(solution)/shard_map/pallas_call | solution.py:89
  141.2 2.9 %collective-permute-done.7.local = bf16[3,8,16384]{2,1,0:T(8,128)(2,1)} collective-permute-done((bf16[3,8,16384]{2,1,0:T(8,128)(2,1)}, bf16[3,8,16384]{2,1,0:T(8,128)(2,1)}, u32[]{:S(2)}, u32[]{:S(2)}) %collective-permute-start.7) | collective-permute-done | bytes 786464 | tf_op jit(solution)/shard_map/ppermute | solution.py:219
  144.0 3.9 %shard_map.88.rest_1_ = bf16[8,32,16384]{2,1,0:T(8,128)(2,1)} custom-call(s32[6]{0:T(128)} %stack.68.table, s32[8]{0:T(128)} %get-tuple-element.15.buffer_rows, f32[8]{0:T(128)} %subtract_divide_fusion.fractions, bf16[8,32,16384]{2,1,0:T(8,128)(2,1)} %points.7, bf16[1,16,16384]{2,1,0:T(8,128)(2,1)} %copy-done, ...), custom_call_target="tpu_custom_call", output_to_operand_aliasing={{}: (8, {})} | custom-call | flops 4194304 | bytes 5767168 | tf_op jit(solution)/shard_map/pallas_call | solution.py:89
  147.9 7.1 %collective-permute-done.5.local = bf16[3,8,16384]{2,1,0:T(8,128)(2,1)} collective-permute-done((bf16[3,8,16384]{2,1,0:T(8,128)(2,1)}, bf16[3,8,16384]{2,1,0:T(8,128)(2,1)}, u32[]{:S(2)}, u32[]{:S(2)}) %collective-permute-start.5) | collective-permute-done | bytes 786464 | tf_op jit(solution)/shard_map/ppermute | solution.py:219
  155.1 3.9 %shard_map.89 = bf16[8,32,16384]{2,1,0:T(8,128)(2,1)} custom-call(s32[6]{0:T(128)} %stack.65.table, s32[8]{0:T(128)} %get-tuple-element.15.buffer_rows, f32[8]{0:T(128)} %subtract_divide_fusion.fractions, bf16[8,32,16384]{2,1,0:T(8,128)(2,1)} %points.7, bf16[1,16,16384]{2,1,0:T(8,128)(2,1)} %copy-done, ...), custom_call_target="tpu_custom_call", output_to_operand_aliasing={{}: (7, {})} | custom-call | flops 4194304 | bytes 5767168 | tf_op jit(solution)/shard_map/pallas_call | solution.py:89
  (60 shorter events, 14.0 us)
Async XLA Ops:
  4.0 91.0 %collective-permute-start.13 = (bf16[3,8,16384]{2,1,0:T(8,128)(2,1)}, bf16[3,8,16384]{2,1,0:T(8,128)(2,1)}, u32[]{:S(2)}, u32[]{:S(2)}) collective-permute-start(bf16[3,8,16384]{2,1,0:T(8,128)(2,1)} %get-tuple-element.5), channel_id=1, source_target_pairs={{4,0},{12,8},{16,20},{24,28},{5,1},{13,9},{17,21},{25,29},{6,2},{1... | collective-permute-start | bytes 2359304 | tf_op jit(solution)/shard_map/ppermute | solution.py:218
  5.3 110.9 %collective-permute-start.12 = (bf16[3,8,16384]{2,1,0:T(8,128)(2,1)}, bf16[3,8,16384]{2,1,0:T(8,128)(2,1)S(1)}, u32[]{:S(2)}, u32[]{:S(2)}) collective-permute-start(bf16[3,8,16384]{2,1,0:T(8,128)(2,1)} %get-tuple-element.5), channel_id=1, source_target_pairs={{20,24},{8,4},{21,25},{9,5},{22,26},{10,6},{23,27},{11,7}} | collective-permute-start | bytes 2359304 | tf_op jit(solution)/shard_map/ppermute | solution.py:222
  6.0 86.6 %collective-permute-start.16 = (bf16[3,8,16384]{2,1,0:T(8,128)(2,1)S(1)}, bf16[3,8,16384]{2,1,0:T(8,128)(2,1)}, u32[]{:S(2)}, u32[]{:S(2)}) collective-permute-start(bf16[3,8,16384]{2,1,0:T(8,128)(2,1)S(1)} %get-tuple-element.4), channel_id=1, source_target_pairs={{4,0},{12,8},{20,16},{8,12},{16,20},{24,28},{5,1},{13,9},{21,17},{... | collective-permute-start | bytes 2359304 | tf_op jit(solution)/shard_map/ppermute | solution.py:218
  9.6 23.1 %collective-permute-start = (bf16[1,16,16384]{2,1,0:T(8,128)(2,1)}, bf16[1,16,16384]{2,1,0:T(8,128)(2,1)S(1)}, u32[]{:S(2)}, u32[]{:S(2)}) collective-permute-start(bf16[1,16,16384]{2,1,0:T(8,128)(2,1)} %get-tuple-element.13), channel_id=1, source_target_pairs={{4,8},{12,16},{20,24},{8,4},{16,12},{24,20},{5,9},{13,17},{21,25},... | collective-permute-start | bytes 1572872 | tf_op jit(solution)/shard_map/ppermute | solution.py:196
  10.3 44.6 %collective-permute-start.1 = (bf16[1,16,16384]{2,1,0:T(8,128)(2,1)}, bf16[1,16,16384]{2,1,0:T(8,128)(2,1)S(1)}, u32[]{:S(2)}, u32[]{:S(2)}) collective-permute-start(bf16[1,16,16384]{2,1,0:T(8,128)(2,1)} %get-tuple-element.12), channel_id=1, source_target_pairs={{0,4},{8,12},{16,20},{24,28},{4,0},{12,8},{20,16},{28,24},{1,5},{9... | collective-permute-start | bytes 1572872 | tf_op jit(solution)/shard_map/ppermute | solution.py:197
  22.9 7.9 %copy-start.9 = (s32[8]{0:T(128)S(1)}, s32[8]{0:T(128)}, u32[]{:S(2)}) copy-start(s32[8]{0:T(128)} %constant.98.clone) | copy-start | bytes 100
  22.9 8.5 %copy-start.8 = (s32[8]{0:T(128)S(1)}, s32[8]{0:T(128)}, u32[]{:S(2)}) copy-start(s32[8]{0:T(128)} %constant.99.clone) | copy-start | bytes 100
  22.9 9.1 %copy-start.7 = (s32[8]{0:T(128)S(1)}, s32[8]{0:T(128)}, u32[]{:S(2)}) copy-start(s32[8]{0:T(128)} %constant.100.clone) | copy-start | bytes 100
  22.9 74.9 %copy-start.5 = (s32[8]{0:T(128)S(1)}, s32[8]{0:T(128)}, u32[]{:S(2)}) copy-start(s32[8]{0:T(128)} %param.8) | copy-start | bytes 100
  22.9 109.3 %copy-start.6 = (s32[8]{0:T(128)S(1)}, s32[8]{0:T(128)}, u32[]{:S(2)}) copy-start(s32[8]{0:T(128)} %param.9) | copy-start | bytes 100
  32.6 104.6 %copy-start = (bf16[1,16,16384]{2,1,0:T(8,128)(2,1)}, bf16[1,16,16384]{2,1,0:T(8,128)(2,1)S(1)}, u32[]{:S(2)}) copy-start(bf16[1,16,16384]{2,1,0:T(8,128)(2,1)S(1)} %collective-permute-done.edge) | copy-start | bytes 1572868
  32.6 56.4 %collective-permute-start.15 = (bf16[2,8,16384]{2,1,0:T(8,128)(2,1)S(1)}, bf16[2,8,16384]{2,1,0:T(8,128)(2,1)}, u32[]{:S(2)}, u32[]{:S(2)}) collective-permute-start(bf16[2,8,16384]{2,1,0:T(8,128)(2,1)S(1)} %get-tuple-element.8), channel_id=1, source_target_pairs={{0,4},{8,12},{16,20},{24,28},{4,0},{12,8},{20,16},{28,24},{1,5},{9... | collective-permute-start | bytes 1572872 | tf_op jit(solution)/shard_map/ppermute | solution.py:219
  54.9 78.4 %copy-start.1 = (bf16[1,16,16384]{2,1,0:T(8,128)(2,1)}, bf16[1,16,16384]{2,1,0:T(8,128)(2,1)S(1)}, u32[]{:S(2)}) copy-start(bf16[1,16,16384]{2,1,0:T(8,128)(2,1)S(1)} %collective-permute-done.1.edge) | copy-start | bytes 1572868
  65.1 15.4 %collective-permute-start.2 = (f32[65]{0:T(128)S(1)}, f32[65]{0:T(128)S(1)}, u32[]{:S(2)}, u32[]{:S(2)}) collective-permute-start(f32[65]{0:T(128)S(1)} %dynamic_update_slice.5), channel_id=1, source_target_pairs={{0,24},{8,0},{16,8},{24,16},{4,12},{12,20},{20,28},{28,4},{1,25},{... | collective-permute-start | bytes 788 | tf_op jit(solution)/shard_map/ppermute | solution.py:243
  80.6 4.5 %collective-permute-start.3 = (f32[65]{0:T(128)S(1)}, f32[65]{0:T(128)S(1)}, u32[]{:S(2)}, u32[]{:S(2)}) collective-permute-start(f32[65]{0:T(128)S(1)} %add_dynamic-update-slice_fusion), channel_id=1, source_target_pairs={{0,16},{8,24},{16,0},{24,8},{4,20},{12,28},{20,4},{28,12},{1,17},{... | collective-permute-start | bytes 788 | tf_op jit(solution)/shard_map/ppermute | solution.py:243
  85.0 6.3 %collective-permute-start.4 = (f32[65]{0:T(128)S(1)}, f32[65]{0:T(128)S(1)}, u32[]{:S(2)}, u32[]{:S(2)}) collective-permute-start(f32[65]{0:T(128)S(1)} %add.85), channel_id=1, source_target_pairs={{0,28},{8,4},{16,12},{24,20},{4,8},{12,16},{20,24},{28,0},{1,29},{... | collective-permute-start | bytes 788 | tf_op jit(solution)/shard_map/ppermute | solution.py:247
  89.0 15.1 %collective-permute-start.11 = (bf16[2,8,16384]{2,1,0:T(8,128)(2,1)}, bf16[2,8,16384]{2,1,0:T(8,128)(2,1)}, u32[]{:S(2)}, u32[]{:S(2)}) collective-permute-start(bf16[2,8,16384]{2,1,0:T(8,128)(2,1)} %get-tuple-element.9), channel_id=1, source_target_pairs={{0,4},{8,12},{16,20},{24,28},{4,0},{12,8},{20,16},{28,24},{1,5},{9... | collective-permute-start | bytes 1572872 | tf_op jit(solution)/shard_map/ppermute | solution.py:219
  91.3 24.1 %collective-permute-start.9 = (bf16[2,8,16384]{2,1,0:T(8,128)(2,1)}, bf16[2,8,16384]{2,1,0:T(8,128)(2,1)}, u32[]{:S(2)}, u32[]{:S(2)}) collective-permute-start(bf16[2,8,16384]{2,1,0:T(8,128)(2,1)} %get-tuple-element.10), channel_id=1, source_target_pairs={{4,0},{24,28},{5,1},{25,29},{6,2},{26,30},{7,3},{27,31}} | collective-permute-start | bytes 1572872 | tf_op jit(solution)/shard_map/ppermute | solution.py:218
  92.6 25.1 %collective-permute-start.17 = (bf16[3,8,16384]{2,1,0:T(8,128)(2,1)}, bf16[3,8,16384]{2,1,0:T(8,128)(2,1)S(1)}, u32[]{:S(2)}, u32[]{:S(2)}) collective-permute-start(bf16[3,8,16384]{2,1,0:T(8,128)(2,1)} %collective-permute-done.16), channel_id=1, source_target_pairs={{0,8},{8,16},{16,24},{12,4},{20,12},{28,20},{1,9},{9,17},{17,25},{... | collective-permute-start | bytes 2359304 | tf_op jit(solution)/shard_map/ppermute | solution.py:224
  95.0 30.2 %collective-permute-start.14 = (bf16[3,8,16384]{2,1,0:T(8,128)(2,1)}, bf16[3,8,16384]{2,1,0:T(8,128)(2,1)S(1)}, u32[]{:S(2)}, u32[]{:S(2)}) collective-permute-start(bf16[3,8,16384]{2,1,0:T(8,128)(2,1)} %collective-permute-done.13), channel_id=1, source_target_pairs={{0,8},{8,16},{20,12},{28,20},{1,9},{9,17},{21,13},{29,21},{2,10},{... | collective-permute-start | bytes 2359304 | tf_op jit(solution)/shard_map/ppermute | solution.py:224
  104.1 39.9 %collective-permute-start.7 = (bf16[3,8,16384]{2,1,0:T(8,128)(2,1)}, bf16[3,8,16384]{2,1,0:T(8,128)(2,1)}, u32[]{:S(2)}, u32[]{:S(2)}) collective-permute-start(bf16[3,8,16384]{2,1,0:T(8,128)(2,1)} %get-tuple-element.6), channel_id=1, source_target_pairs={{0,4},{8,12},{16,20},{24,28},{4,0},{12,8},{20,16},{28,24},{1,5},{9... | collective-permute-start | bytes 2359304 | tf_op jit(solution)/shard_map/ppermute | solution.py:219
  115.4 39.7 %collective-permute-start.5 = (bf16[3,8,16384]{2,1,0:T(8,128)(2,1)}, bf16[3,8,16384]{2,1,0:T(8,128)(2,1)}, u32[]{:S(2)}, u32[]{:S(2)}) collective-permute-start(bf16[3,8,16384]{2,1,0:T(8,128)(2,1)} %get-tuple-element.7), channel_id=1, source_target_pairs={{0,4},{8,12},{16,20},{24,28},{4,0},{12,8},{20,16},{28,24},{1,5},{9... | collective-permute-start | bytes 2359304 | tf_op jit(solution)/shard_map/ppermute | solution.py:219
  116.2 21.0 %copy-start.2 = (bf16[3,8,16384]{2,1,0:T(8,128)(2,1)}, bf16[3,8,16384]{2,1,0:T(8,128)(2,1)S(1)}, u32[]{:S(2)}) copy-start(bf16[3,8,16384]{2,1,0:T(8,128)(2,1)S(1)} %collective-permute-done.12.rest_0_) | copy-start | bytes 2359300
  116.2 24.9 %collective-permute-start.8 = (bf16[2,8,16384]{2,1,0:T(8,128)(2,1)}, bf16[2,8,16384]{2,1,0:T(8,128)(2,1)}, u32[]{:S(2)}, u32[]{:S(2)}) collective-permute-start(bf16[2,8,16384]{2,1,0:T(8,128)(2,1)} %get-tuple-element.10), channel_id=1, source_target_pairs={{12,16},{20,24},{8,4},{16,12},{13,17},{21,25},{9,5},{17,13},{14,18... | collective-permute-start | bytes 1572872 | tf_op jit(solution)/shard_map/ppermute | solution.py:222
  117.7 15.7 %copy-start.3 = (bf16[3,8,16384]{2,1,0:T(8,128)(2,1)}, bf16[3,8,16384]{2,1,0:T(8,128)(2,1)S(1)}, u32[]{:S(2)}) copy-start(bf16[3,8,16384]{2,1,0:T(8,128)(2,1)S(1)} %collective-permute-done.17.rest_0_) | copy-start | bytes 2359300
  117.7 30.2 %collective-permute-start.6 = (bf16[2,8,16384]{2,1,0:T(8,128)(2,1)}, bf16[2,8,16384]{2,1,0:T(8,128)(2,1)}, u32[]{:S(2)}, u32[]{:S(2)}) collective-permute-start(bf16[2,8,16384]{2,1,0:T(8,128)(2,1)} %get-tuple-element.11), channel_id=1, source_target_pairs={{4,8},{12,16},{20,24},{8,4},{16,12},{24,20},{5,9},{13,17},{21,25},... | collective-permute-start | bytes 1572872 | tf_op jit(solution)/shard_map/ppermute | solution.py:222
  125.3 12.0 %copy-start.4 = (bf16[3,8,16384]{2,1,0:T(8,128)(2,1)}, bf16[3,8,16384]{2,1,0:T(8,128)(2,1)S(1)}, u32[]{:S(2)}) copy-start(bf16[3,8,16384]{2,1,0:T(8,128)(2,1)S(1)} %collective-permute-done.14.rest_1_) | copy-start | bytes 2359300
  125.3 18.8 %collective-permute-start.10 = (bf16[2,8,16384]{2,1,0:T(8,128)(2,1)}, bf16[2,8,16384]{2,1,0:T(8,128)(2,1)}, u32[]{:S(2)}, u32[]{:S(2)}) collective-permute-start(bf16[2,8,16384]{2,1,0:T(8,128)(2,1)} %collective-permute-done.9), channel_id=1, source_target_pairs={{0,8},{28,20},{1,9},{29,21},{2,10},{30,22},{3,11},{31,23}} | collective-permute-start | bytes 1572872 | tf_op jit(solution)/shard_map/ppermute | solution.py:224

commit v3 on v2

v3 whole, which is shorter than its diff:
```python
import functools

import jax
import jax.numpy as jnp
import numpy as np
from jax import lax
from jax.experimental import pallas as pl
from jax.experimental.pallas import tpu as pltpu
from jax.sharding import PartitionSpec as P


BLOCK_COLS = 1024
LOW = 3
HIGH = 3
CHAIN_CHUNKS = 4
CUTS = (0, 2, 4, 7, 8)
COL, EDGE_COL, AT_LOCAL, AT_EDGE, AT_FAR, EDGE_IS_NEXT, RELAYED = range(7)


def place_kernel(
    cols, n_edges, n_fars, has_prev, table, buffer_rows, fractions, points, local, *rest
):
    edges, fars = rest[:n_edges], rest[n_edges : n_edges + n_fars]
    out, buf, res, in_sem, out_sem = rest[n_edges + n_fars + has_prev :]
    n_own = points.shape[0]
    width = min(BLOCK_COLS, cols)
    blocks = cols // width
    col = pl.multiple_of(table[COL], width)
    edge_col = pl.multiple_of(table[EDGE_COL], width)

    def into(src, start, count, c, k):
        dst = buf.at[pl.ds(start, count), :, pl.ds(c * width, width)]
        return pltpu.make_async_copy(src, dst, in_sem.at[c, k])

    def own_in(c):
        at = pl.ds(col + c * width, width)
        return into(points.at[:, :, at], LOW, n_own, c, 0)

    def local_in(c):
        at = pl.ds(c * width, width)
        return into(local.at[:, :, at], table[AT_LOCAL], local.shape[0], c, 1)

    def edge_in(c, edge):
        at = pl.ds(edge_col + c * width, width)
        return into(edge.at[:, :, at], table[AT_EDGE], 1, c, 2)

    def far_in(c, far):
        at = pl.ds(c * width, width)
        return into(far.at[:, :, at], table[AT_FAR], far.shape[0], c, 3)

    def start_one(copy, c, refs, entry):
        if len(refs) == 1:
            copy(c, refs[0]).start()
            return

        @pl.when(table[entry] == 0)
        def _():
            copy(c, refs[0]).start()

        @pl.when(table[entry] == 1)
        def _():
            copy(c, refs[1]).start()

    def res_out(c):
        return pltpu.make_async_copy(
            res.at[:, :, pl.ds(c * width, width)],
            out.at[:, :, pl.ds(col + c * width, width)],
            out_sem.at[c],
        )

    for c in range(blocks):
        own_in(c).start()
        local_in(c).start()
        start_one(edge_in, c, edges, EDGE_IS_NEXT)
        start_one(far_in, c, fars, RELAYED)
    for c in range(blocks):
        own_in(c).wait()
        local_in(c).wait()
        edge_in(c, edges[0]).wait()
        far_in(c, fars[0]).wait()
        at = pl.ds(c * width, width)

        @pl.loop(0, n_own)
        def _(j):
            start = buf[buffer_rows[j], :, at].astype(jnp.float32)
            end = buf[buffer_rows[j] + 1, :, at].astype(jnp.float32)
            res[j, :, at] = (start + fractions[j] * (end - start)).astype(res.dtype)

        res_out(c).start()
    for c in range(blocks):
        res_out(c).wait()


def place(cols, table, buffer_rows, fractions, points, local, edges, fars, prev):
    n_own, rows, _ = points.shape
    held = LOW + n_own + HIGH
    hbm = pl.BlockSpec(memory_space=pl.ANY)
    smem = pl.BlockSpec(memory_space=pltpu.SMEM)
    args = [table, buffer_rows, fractions, points, local, *edges, *fars]
    if prev is not None:
        args.append(prev)
    moved = (held + n_own) * rows * cols * points.dtype.itemsize
    blocks = cols // min(BLOCK_COLS, cols)
    return pl.pallas_call(
        functools.partial(
            place_kernel, cols, len(edges), len(fars), prev is not None
        ),
        out_shape=jax.ShapeDtypeStruct(points.shape, points.dtype),
        in_specs=[smem] * 3 + [hbm] * (len(args) - 3),
        out_specs=hbm,
        scratch_shapes=[
            pltpu.VMEM((held, rows, cols), points.dtype),
            pltpu.VMEM((n_own, rows, cols), points.dtype),
            pltpu.SemaphoreType.DMA((blocks, 4)),
            pltpu.SemaphoreType.DMA((blocks,)),
        ],
        input_output_aliases={} if prev is None else {len(args) - 1: 0},
        cost_estimate=pl.CostEstimate(
            flops=4 * n_own * rows * cols, bytes_accessed=moved, transcendentals=0
        ),
        compiler_params=pltpu.CompilerParams(vmem_limit_bytes=moved + (4 << 20)),
    )(*args)


def squares(start, end):
    step = end.astype(jnp.float32) - start.astype(jnp.float32)
    return jnp.sum(step * step, axis=(1, 2))


def finish(all_squares, first_point, n_own, n_points, source_segment, numerators):
    index = jnp.arange(n_points, dtype=jnp.int32)
    lengths = jnp.where(index < n_points - 1, jnp.sqrt(all_squares), 0.0)
    arcs = jnp.concatenate([jnp.zeros((1,), jnp.float32), jnp.cumsum(lengths)[:-1]])
    total = arcs[n_points - 1]
    target = total * (
        source_segment.astype(jnp.float32) + numerators.astype(jnp.float32) / 65536.0
    ) / (n_points - 1)
    fractions = (target - arcs[source_segment]) / lengths[source_segment]
    arc = lax.dynamic_slice(arcs, (first_point,), (n_own,)) / total
    return fractions, arc


def chain_device(points, source_segment, numerators):
    n_own, _, width = points.shape
    device_index = lax.axis_index("seg")
    device_count = lax.axis_size("seg")
    first_point = device_index * n_own
    n_points = device_count * n_own
    forward = [(i, i + 1) for i in range(device_count - 1)]
    backward = [(b, a) for a, b in forward]
    cols = width // CHAIN_CHUNKS

    first = lax.ppermute(points[:1], "seg", backward)
    lows, highs = [], []
    for c in range(CHAIN_CHUNKS):
        at = slice(c * cols, (c + 1) * cols)
        lows.append(lax.ppermute(points[n_own - LOW :, :, at], "seg", forward))
        highs.append(lax.ppermute(points[1:HIGH, :, at], "seg", backward))
    inner = squares(points[:-1], points[1:])
    edge = squares(points[n_own - 1 :], first)
    own_squares = lax.psum(jnp.concatenate([inner, edge]), "par")
    all_squares = lax.all_gather(own_squares, "seg", axis=0, tiled=True)
    fractions, arc = finish(
        all_squares, first_point, n_own, n_points, source_segment, numerators
    )
    buffer_rows = source_segment - first_point + LOW
    out = None
    for c in range(CHAIN_CHUNKS):
        table = jnp.array(
            [c * cols, c * cols, 0, LOW + n_own, LOW + n_own + 1, 0, 0], jnp.int32
        )
        out = place(
            cols, table, buffer_rows, fractions, points, lows[c],
            (first,), (highs[c],), out,
        )
    return (out, arc)


def paired_device(points, source_segment, numerators):
    n_own, _, width = points.shape
    device_index = lax.axis_index("seg")
    count = lax.axis_size("seg")
    pairs = count // 2
    even = device_index % 2 == 0
    first_point = device_index * n_own
    n_points = count * n_own
    steps = len(CUTS) - 1
    half = width // 2
    cuts = [width * cut // CUTS[-1] for cut in CUTS]

    forward = [(i, i + 1) for i in range(count - 1)]
    backward = [(b, a) for a, b in forward]
    local_pairs = [(2 * k, 2 * k + 1) for k in range(pairs)]
    local_pairs += [(b, a) for a, b in local_pairs]
    far_pairs = [(2 * k + 1, 2 * k + 2) for k in range(pairs - 1)]
    far_pairs += [(b, a) for a, b in far_pairs]

    def relayed(source, step):
        k = source // 2 if source % 2 == 0 else pairs - 1 - source // 2
        return k * steps > step * pairs

    def beside(source):
        return source + 1 if source % 2 == 0 else source - 1

    hop1, hop2, direct = [], [], []
    for s in range(steps):
        through = [(a, b) for a, b in far_pairs if relayed(a, s)]
        hop1.append([(a, beside(a)) for a, b in through])
        hop2.append([(beside(a), b) for a, b in through])
        direct.append([(a, b) for a, b in far_pairs if not relayed(a, s)])

    from_prev = lax.ppermute(points[n_own - 1 :, :, half:], "seg", forward)
    from_next = lax.ppermute(points[:1, :, :half], "seg", backward)

    def span(to_even, step):
        start, end = cuts[step], cuts[step + 1]
        return slice(start, end) if to_even else slice(width - end, width - start)

    far_payload, local_payload = [], []
    for s in range(steps):
        n_far = 3 if s < steps // 2 else 2
        n_local = 5 - n_far
        on, back = span(True, s), span(False, s)
        far_payload.append(
            jnp.where(
                even,
                points[3 - n_far : 3, :, back],
                points[n_own - 3 : n_own - 3 + n_far, :, on],
            )
        )
        local_payload.append(
            jnp.where(
                even,
                points[n_own - 3 : n_own - 3 + n_local, :, back],
                points[3 - n_local : 3, :, on],
            )
        )
    middle, relay, far, local = {}, {}, {}, {}
    for s in range(steps):
        if hop1[s]:
            middle[s] = lax.ppermute(far_payload[s], "seg", hop1[s])
        local[s] = lax.ppermute(local_payload[s], "seg", local_pairs)
    for s in range(steps):
        if direct[s]:
            far[s] = lax.ppermute(far_payload[s], "seg", direct[s])
        if hop2[s]:
            relay[s] = lax.ppermute(middle[s], "seg", hop2[s])

    partial = jnp.concatenate(
        [
            squares(from_prev, points[:1, :, half:]),
            squares(points[:-1], points[1:]),
            squares(points[n_own - 1 :, :, :half], from_next),
        ]
    )
    partial = lax.psum(partial, "par")
    spread = lax.dynamic_update_slice(
        jnp.zeros((n_points + 1,), jnp.float32), partial, (first_point,)
    )
    shift = 1
    while shift < pairs:
        ring = [(2 * k, 2 * ((k - shift) % pairs)) for k in range(pairs)]
        ring += [(2 * k + 1, 2 * ((k + shift) % pairs) + 1) for k in range(pairs)]
        spread = spread + lax.ppermute(spread, "seg", ring)
        shift *= 2
    cross = [(2 * k, 2 * ((k - 1) % pairs) + 1) for k in range(pairs)]
    cross += [(2 * k + 1, 2 * ((k + 1) % pairs)) for k in range(pairs)]
    spread = spread + lax.ppermute(spread, "seg", cross)
    fractions, arc = finish(
        spread[1:], first_point, n_own, n_points, source_segment, numerators
    )
    buffer_rows = source_segment - first_point + LOW

    tables = np.zeros((count, steps, 7), np.int32)
    for s in range(steps):
        early = s < steps // 2
        for i in range(count):
            at_even = i % 2 == 0
            col = span(at_even, s).start
            next_edge = at_even == early
            tables[i, s, COL] = col
            tables[i, s, EDGE_COL] = col % half
            tables[i, s, EDGE_IS_NEXT] = next_edge
            tables[i, s, AT_EDGE] = LOW + n_own if next_edge else LOW - 1
            tables[i, s, AT_LOCAL] = LOW + n_own + early if at_even else 0
            tables[i, s, AT_FAR] = 0 if at_even else LOW + n_own + (not early)
        for _, b in hop2[s]:
            tables[b, s, RELAYED] = 1
    table = lax.dynamic_index_in_dim(jnp.asarray(tables), device_index, 0, False)
    out = None
    for s in range(steps):
        fars = tuple(d[s] for d in (far, relay) if s in d)
        out = place(
            cuts[s + 1] - cuts[s], table[s], buffer_rows, fractions,
            points, local[s], (from_prev, from_next), fars, out,
        )
    return (out, arc)


def is_paired(mesh):
    names = mesh.axis_names
    devices = np.moveaxis(mesh.devices, names.index("seg"), 0)
    devices = devices.reshape(devices.shape[0], -1)[:, 0]
    count = len(devices)
    pairs = count // 2
    if count % 2 or pairs != len(CUTS) - 1:
        return False
    places = [getattr(device, "coords", None) for device in devices]
    if any(place is None for place in places):
        return False
    return all(
        (place[0], place[2]) == (i % 2, i // 2) and place[1] == places[0][1]
        for i, place in enumerate(places)
    )


def solution(mesh):
    paired = is_paired(mesh)

    def body(*args):
        return (paired_device if paired else chain_device)(*args)

    return jax.shard_map(
        body,
        mesh=mesh,
        in_specs=(P("seg", "par", None), P("seg"), P("seg")),
        out_specs=(P("seg", "par", None), P("seg")),
        check_vma=False,
    )
```

time: 160 us -> 161 us (level)
  waiting for transfers between devices: 56.4 us -> 32.6 us
  other arithmetic: 14.8 us -> 34.2 us
  starting transfers between devices: 48.4 us -> 54.5 us
    select_n x0 -> x6, other arithmetic: none -> 13.6 us  [the longest x3 7.27 us: paired_device(): jnp.where(even, points[3 - n_far:3, :, back], points[n_own - 3:n_own - 3...]
    ppermute x3, waiting for transfers between devices: 11.2 us -> 0.01 us  [paired_device(): middle[s] = lax.ppermute(far_payload[s], 'seg', hop1[s])]
    ppermute x4, waiting for transfers between devices: 14.9 us -> 4.96 us  [paired_device(): local[s] = lax.ppermute(local_payload[s], 'seg', local_pairs)]
    dynamic_slice x6 -> x1, local copies, waits for them, and re-layouts: 10.2 us -> 0.69 us  [paired_device(): lax.dynamic_index_in_dim(jnp.asarray(tables), device_index, 0, False)]
    ppermute x2, waiting for transfers between devices: 12.1 us -> 2.92 us  [the longest x1 2.92 us: paired_device(): from_prev = lax.ppermute(points[n_own - 1:, :, half:], 'seg', forward)]
    ppermute x3, waiting for transfers between devices: 6.08 us -> 14.7 us  [paired_device(): relay[s] = lax.ppermute(middle[s], 'seg', hop2[s])]
    unnamed x20 -> x18, local copies, waits for them, and re-layouts: 0.04 us -> 5.27 us
    another operation x4 -> x0, local copies, waits for them, and re-layouts: 4.33 us -> none  [paired_device(): jnp.stack([row, row % half, at_local, at_edge, at_far, flag])]
  transfers between devices with their start and end apart: 18 -> 18, of which waited for: 9 -> 5; matrix products, arithmetic and copies ran while one was open for 18% -> 26% of each run, Pallas kernels for 7% -> 7%
where the time goes in v3:
time: 161 us; the launch traced here: 159 us
  starting transfers between devices  54.5 us (34%)
  other arithmetic  34.2 us (21%)
  waiting for transfers between devices  32.6 us (20%)
  local copies, waits for them, and re-layouts  16 us (10%)
  Pallas kernels  14.4 us (9%)
  blocking collectives  6.19 us (4%)
    ppermute x3, waiting for transfers between devices, paired_device(): relay[s] = lax.ppermute(middle[s], 'seg', hop2[s])  14.7 us
    ppermute x4, starting transfers between devices, paired_device(): local[s] = lax.ppermute(local_payload[s], 'seg', local_pairs)  14.5 us
    pallas_call x4, Pallas kernels, place(): pl.pallas_call(functools.partial(place_kernel, cols, len(edges), len(fars...  14.4 us
    ppermute x3, starting transfers between devices, paired_device(): relay[s] = lax.ppermute(middle[s], 'seg', hop2[s])  11.8 us
    reduce_sum x2, other arithmetic, squares(): return jnp.sum(step * step, axis=(1, 2))  9.98 us
    ppermute x2, waiting for transfers between devices, paired_device(): spread = spread + lax.ppermute(spread, 'seg', ring)  8.8 us
    ppermute x2, starting transfers between devices, paired_device(): spread = spread + lax.ppermute(spread, 'seg', ring)  7.96 us
    select_n x3, other arithmetic, paired_device(): jnp.where(even, points[3 - n_far:3, :, back], points[n_own - 3:n_own - 3...  7.27 us
  transfers between devices with their start and end apart: 18, of which 5 were waited for; matrix products, arithmetic and copies ran while one was open for 26% of the time, Pallas kernels for 7%

profile of v3, /device:TPU:0, one launch (start us, length us, event | category | flops | bytes accessed | tf_op | source)
XLA Modules:
  0.0 158.7 jit_solution(8412444436853124615)
XLA Ops:
  0.6 3.2 %slice_select_fusion.1 = (bf16[3,32,4096]{2,1,0:T(8,128)(2,1)}, bf16[3,32,4096]{2,1,0:T(8,128)(2,1)}) fusion(bf16[8,32,16384]{2,1,0:T(8,128)(2,1)} %points.7, pred[]{:T(512)S(6)} %eq.5), kind=kLoop, calls=%fused_computation.6 | loop fusion | flops 786432 | bytes 4718593 | tf_op jit(solution)/shard_map/jit(_where)/select_n | solution.py:225
  5.1 2.1 %fusion = (bf16[1,32,8192]{2,1,0:T(8,128)(2,1)}, bf16[1,32,8192]{2,1,0:T(8,128)(2,1)S(1)}) fusion(bf16[8,32,16384]{2,1,0:T(8,128)(2,1)} %points.7), kind=kLoop, calls=%fused_computation.28 | loop fusion | bytes 2097152 | tf_op jit(solution)/shard_map/slice | solution.py:213
  7.2 5.8 %collective-permute-start = (bf16[1,32,8192]{2,1,0:T(8,128)(2,1)S(1)}, bf16[1,32,8192]{2,1,0:T(8,128)(2,1)S(1)}, u32[]{:S(2)}, u32[]{:S(2)}) collective-permute-start(bf16[1,32,8192]{2,1,0:T(8,128)(2,1)S(1)} %get-tuple-element.9), channel_id=1, source_target_pairs={{0,4},{4,8},{8,12},{12,16},{16,20},{20,24},{24,28},{1,5},{5,9},{9,... | collective-permute-start | bytes 1572872 | tf_op jit(solution)/shard_map/ppermute | solution.py:212
  14.2 1.6 %slice_select_fusion.4 = (bf16[2,32,4096]{2,1,0:T(8,128)(2,1)S(1)}, bf16[2,32,4096]{2,1,0:T(8,128)(2,1)S(1)}) fusion(bf16[8,32,16384]{2,1,0:T(8,128)(2,1)} %points.7, pred[]{:T(512)S(6)} %eq.5), kind=kLoop, calls=%fused_computation.9 | loop fusion | flops 524288 | bytes 3145729 | tf_op jit(solution)/shard_map/jit(_where)/select_n | solution.py:232
  15.9 3.4 %collective-permute-start.15 = (bf16[2,32,4096]{2,1,0:T(8,128)(2,1)S(1)}, bf16[2,32,4096]{2,1,0:T(8,128)(2,1)S(1)}, u32[]{:S(2)}, u32[]{:S(2)}) collective-permute-start(bf16[2,32,4096]{2,1,0:T(8,128)(2,1)S(1)} %get-tuple-element.6), channel_id=1, source_target_pairs={{0,4},{8,12},{16,20},{24,28},{4,0},{12,8},{20,16},{28,24},{1,5},{9... | collective-permute-start | bytes 1572872 | tf_op jit(solution)/shard_map/ppermute | solution.py:242
  20.6 2.3 %slice_select_fusion.3 = bf16[2,32,6144]{2,1,0:T(8,128)(2,1)} fusion(bf16[8,32,16384]{2,1,0:T(8,128)(2,1)} %points.7, pred[]{:T(512)S(6)} %eq.5), kind=kLoop, calls=%fused_computation.8 | loop fusion | flops 393216 | bytes 2359297 | tf_op jit(solution)/shard_map/jit(_where)/select_n | solution.py:225
  23.0 2.8 %slice_select_fusion = bf16[3,32,6144]{2,1,0:T(8,128)(2,1)} fusion(bf16[8,32,16384]{2,1,0:T(8,128)(2,1)} %points.7, pred[]{:T(512)S(6)} %eq.5), kind=kLoop, calls=%fused_computation.3 | loop fusion | flops 589824 | bytes 3538945 | tf_op jit(solution)/shard_map/jit(_where)/select_n | solution.py:232
  25.7 7.8 %multiply_reduce_fusion = f32[7]{0:T(128)S(1)} fusion(bf16[8,32,16384]{2,1,0:T(8,128)(2,1)} %points.7), kind=kLoop, calls=%fused_computation.2 | loop fusion | flops 18350072 | bytes 14680092 | tf_op jit(solution)/shard_map/reduce_sum | solution.py:127
  33.5 2.9 %collective-permute-done.rest_0_ = bf16[1,32,8192]{2,1,0:T(8,128)(2,1)S(1)} collective-permute-done((bf16[1,32,8192]{2,1,0:T(8,128)(2,1)S(1)}, bf16[1,32,8192]{2,1,0:T(8,128)(2,1)S(1)}, u32[]{:S(2)}, u32[]{:S(2)}) %collective-permute-start) | collective-permute-done | bytes 524320 | tf_op jit(solution)/shard_map/ppermute | solution.py:212
  36.4 2.5 %collective-permute-start.11 = (bf16[2,32,4096]{2,1,0:T(8,128)(2,1)S(1)}, bf16[2,32,4096]{2,1,0:T(8,128)(2,1)S(1)}, u32[]{:S(2)}, u32[]{:S(2)}) collective-permute-start(bf16[2,32,4096]{2,1,0:T(8,128)(2,1)S(1)} %get-tuple-element.7), channel_id=1, source_target_pairs={{0,4},{8,12},{16,20},{24,28},{4,0},{12,8},{20,16},{28,24},{1,5},{9... | collective-permute-start | bytes 1572872 | tf_op jit(solution)/shard_map/ppermute | solution.py:242
  38.9 2.2 %multiply_reduce_fusion.2 = (f32[]{:T(128)}, f32[]{:T(128)}) fusion(bf16[1,32,8192]{2,1,0:T(8,128)(2,1)S(1)} %collective-permute-done.rest_0_, bf16[8,32,16384]{2,1,0:T(8,128)(2,1)} %points.7, bf16[1,32,8192]{2,1,0:T(8,128)(2,1)S(1)} %collective-permute-done.1.rest_1_), kind=kLoop, calls=%fused_computation.5 | loop fusion | flops 2621438 | bytes 2097160 | tf_op jit(solution)/shard_map/reduce_sum | solution.py:127
  42.5 6.2 %psum.7 = f32[9]{0:T(128)S(1)} all-reduce(f32[9]{0:T(128)S(1)} %pad_maximum_fusion), channel_id=1, replica_groups=mesh['seg'=8,'par'=4] {'par'}, use_global_device_ids=true, to_apply=%region_3.4 | all-reduce | flops 9 | bytes 72 | tf_op jit(solution)/shard_map/psum | solution.py:256
  48.9 4.9 %collective-permute-start.2 = (f32[65]{0:T(128)S(1)}, f32[65]{0:T(128)S(1)}, u32[]{:S(2)}, u32[]{:S(2)}) collective-permute-start(f32[65]{0:T(128)S(1)} %dynamic_update_slice.5), channel_id=1, source_target_pairs={{0,24},{8,0},{16,8},{24,16},{4,12},{12,20},{20,28},{28,4},{1,25},{... | collective-permute-start | bytes 788 | tf_op jit(solution)/shard_map/ppermute | solution.py:264
  53.8 2.0 %slice_select_fusion.6 = bf16[3,32,2048]{2,1,0:T(8,128)(2,1)} fusion(bf16[8,32,16384]{2,1,0:T(8,128)(2,1)} %points.7, pred[]{:T(512)S(6)} %eq.5), kind=kLoop, calls=%fused_computation.11 | loop fusion | flops 196608 | bytes 1179649 | tf_op jit(solution)/shard_map/jit(_where)/select_n | solution.py:232
  55.8 8.8 %collective-permute-done.2 = f32[65]{0:T(128)S(1)} collective-permute-done((f32[65]{0:T(128)S(1)}, f32[65]{0:T(128)S(1)}, u32[]{:S(2)}, u32[]{:S(2)}) %collective-permute-start.2) | collective-permute-done | bytes 292 | tf_op jit(solution)/shard_map/ppermute | solution.py:264
  64.7 3.0 %collective-permute-start.3 = (f32[65]{0:T(128)S(1)}, f32[65]{0:T(128)S(1)}, u32[]{:S(2)}, u32[]{:S(2)}) collective-permute-start(f32[65]{0:T(128)S(1)} %add_dynamic-update-slice_fusion), channel_id=1, source_target_pairs={{0,16},{8,24},{16,0},{24,8},{4,20},{12,28},{20,4},{28,12},{1,17},{... | collective-permute-start | bytes 788 | tf_op jit(solution)/shard_map/ppermute | solution.py:264
  67.8 1.8 %slice_select_fusion.7 = bf16[2,32,2048]{2,1,0:T(8,128)(2,1)} fusion(bf16[8,32,16384]{2,1,0:T(8,128)(2,1)} %points.7, pred[]{:T(512)S(6)} %eq.5), kind=kLoop, calls=%fused_computation.12 | loop fusion | flops 131072 | bytes 786433 | tf_op jit(solution)/shard_map/jit(_where)/select_n | solution.py:225
  72.2 5.0 %collective-permute-done.11.local = bf16[2,32,4096]{2,1,0:T(8,128)(2,1)S(1)} collective-permute-done((bf16[2,32,4096]{2,1,0:T(8,128)(2,1)S(1)}, bf16[2,32,4096]{2,1,0:T(8,128)(2,1)S(1)}, u32[]{:S(2)}, u32[]{:S(2)}) %collective-permute-start.11) | collective-permute-done | bytes 524320 | tf_op jit(solution)/shard_map/ppermute | solution.py:242
  78.0 5.7 %collective-permute-start.4 = (f32[65]{0:T(128)S(1)}, f32[65]{0:T(128)}, u32[]{:S(2)}, u32[]{:S(2)}) collective-permute-start(f32[65]{0:T(128)S(1)} %add.40), channel_id=1, source_target_pairs={{0,28},{8,4},{16,12},{24,20},{4,8},{12,16},{20,24},{28,0},{1,29},{... | collective-permute-start | bytes 788 | tf_op jit(solution)/shard_map/ppermute | solution.py:268
  85.3 8.6 %collective-permute-start.7 = (bf16[3,32,6144]{2,1,0:T(8,128)(2,1)}, bf16[3,32,6144]{2,1,0:T(8,128)(2,1)S(1)}, u32[]{:S(2)}, u32[]{:S(2)}) collective-permute-start(bf16[3,32,6144]{2,1,0:T(8,128)(2,1)} %slice_select_fusion), channel_id=1, source_target_pairs={{0,4},{8,12},{16,20},{24,28},{4,0},{12,8},{20,16},{28,24},{1,5},{9... | collective-permute-start | bytes 3538952 | tf_op jit(solution)/shard_map/ppermute | solution.py:242
  93.9 4.3 %collective-permute-start.17 = (bf16[3,32,4096]{2,1,0:T(8,128)(2,1)}, bf16[3,32,4096]{2,1,0:T(8,128)(2,1)}, u32[]{:S(2)}, u32[]{:S(2)}) collective-permute-start(bf16[3,32,4096]{2,1,0:T(8,128)(2,1)} %collective-permute-done.16), channel_id=1, source_target_pairs={{0,8},{8,16},{16,24},{12,4},{20,12},{28,20},{1,9},{9,17},{17,25},{... | collective-permute-start | bytes 2359304 | tf_op jit(solution)/shard_map/ppermute | solution.py:247
  98.2 5.0 %collective-permute-start.14 = (bf16[3,32,4096]{2,1,0:T(8,128)(2,1)}, bf16[3,32,4096]{2,1,0:T(8,128)(2,1)}, u32[]{:S(2)}, u32[]{:S(2)}) collective-permute-start(bf16[3,32,4096]{2,1,0:T(8,128)(2,1)} %collective-permute-done.13), channel_id=1, source_target_pairs={{0,8},{8,16},{20,12},{28,20},{1,9},{9,17},{21,13},{29,21},{2,10},{... | collective-permute-start | bytes 2359304 | tf_op jit(solution)/shard_map/ppermute | solution.py:247
  110.1 1.6 collective-permute-start.8
  111.6 2.6 %collective-permute-start.10 = (bf16[2,32,6144]{2,1,0:T(8,128)(2,1)}, bf16[2,32,6144]{2,1,0:T(8,128)(2,1)}, u32[]{:S(2)}, u32[]{:S(2)}) collective-permute-start(bf16[2,32,6144]{2,1,0:T(8,128)(2,1)} %collective-permute-done.9), channel_id=1, source_target_pairs={{0,8},{28,20},{1,9},{29,21},{2,10},{30,22},{3,11},{31,23}} | collective-permute-start | bytes 2359304 | tf_op jit(solution)/shard_map/ppermute | solution.py:247
  117.7 14.7 %collective-permute-done.14.rest_3_ = bf16[3,32,4096]{2,1,0:T(8,128)(2,1)} collective-permute-done((bf16[3,32,4096]{2,1,0:T(8,128)(2,1)}, bf16[3,32,4096]{2,1,0:T(8,128)(2,1)}, u32[]{:S(2)}, u32[]{:S(2)}) %collective-permute-start.14) | collective-permute-done | bytes 786464 | tf_op jit(solution)/shard_map/ppermute | solution.py:247
  135.0 1.9 %gather_fusion = f32[8]{0:T(128)} fusion(f32[64]{0:T(128)} %copy-done.4, s32[1024]{0:T(1024)} %pad_clamp_fusion), kind=kCustom, calls=%fused_computation | custom fusion | bytes 96 | tf_op jit(solution)/shard_map/gather | solution.py:138
  136.9 2.0 %gather_fusion.1 = f32[8]{0:T(128)} fusion(f32[64]{0:T(128)} %compare_select_fusion.1, s32[1024]{0:T(1024)} %pad_clamp_fusion), kind=kCustom, calls=%fused_computation.1 | custom fusion | bytes 96 | tf_op jit(solution)/shard_map/gather | solution.py:138
  140.2 3.4 %copy-done = bf16[8,32,16384]{2,1,0:T(8,128)(2,1)S(1)} copy-done((bf16[8,32,16384]{2,1,0:T(8,128)(2,1)S(1)}, bf16[8,32,16384]{2,1,0:T(8,128)(2,1)}, u32[]{:S(2)}) %copy-start) | copy-done | bytes 8388632
  144.2 3.9 %shard_map.59.rest_4_ = bf16[8,32,16384]{2,1,0:T(8,128)(2,1)} custom-call(s32[7]{0:T(128)S(1)} %copy-done.3, s32[8]{0:T(128)S(1)} %get-tuple-element.15.buffer_rows, f32[8]{0:T(128)S(1)} %subtract_divide_fusion.fractions, bf16[8,32,16384]{2,1,0:T(8,128)(2,1)S(1)} %copy-done, bf16[2,32,4096]{2,1,0:T(8,128)(2,1)S(1)} %collective-permute-done.15.local, ...), custom_call_target="tpu_custom_call" | custom-call | flops 4194304 | bytes 5767168 | tf_op jit(solution)/shard_map/pallas_call | solution.py:104
  148.2 3.2 %shard_map.60.rest_4_ = bf16[8,32,16384]{2,1,0:T(8,128)(2,1)} custom-call(s32[7]{0:T(128)S(1)} %get-tuple-element.11.table, s32[8]{0:T(128)S(1)} %get-tuple-element.15.buffer_rows, f32[8]{0:T(128)S(1)} %subtract_divide_fusion.fractions, bf16[8,32,16384]{2,1,0:T(8,128)(2,1)S(1)} %copy-done, ...), custom_call_target="tpu_custom_call", output_to_operand_aliasing={{}: (9, {})} | custom-call | flops 4194304 | bytes 5767168 | tf_op jit(solution)/shard_map/pallas_call | solution.py:104
  151.4 4.2 %shard_map.61.rest_3_ = bf16[8,32,16384]{2,1,0:T(8,128)(2,1)} custom-call(s32[7]{0:T(128)S(1)} %get-tuple-element.12.table, s32[8]{0:T(128)S(1)} %get-tuple-element.15.buffer_rows, f32[8]{0:T(128)S(1)} %subtract_divide_fusion.fractions, bf16[8,32,16384]{2,1,0:T(8,128)(2,1)S(1)} %bitcast.14, ...), custom_call_target="tpu_custom_call", output_to_operand_aliasing={{}: (9, {})} | custom-call | flops 6291456 | bytes 8650752 | tf_op jit(solution)/shard_map/pallas_call | solution.py:104
  155.7 3.0 %shard_map.62 = bf16[8,32,16384]{2,1,0:T(8,128)(2,1)} custom-call(s32[7]{0:T(128)S(1)} %get-tuple-element.13.table, s32[8]{0:T(128)S(1)} %get-tuple-element.15.buffer_rows, f32[8]{0:T(128)S(1)} %subtract_divide_fusion.fractions, bf16[8,32,16384]{2,1,0:T(8,128)(2,1)S(1)} %bitcast.14, ...), custom_call_target="tpu_custom_call", output_to_operand_aliasing={{}: (8, {})} | custom-call | flops 2097152 | bytes 2883584 | tf_op jit(solution)/shard_map/pallas_call | solution.py:104
  (58 shorter events, 25.7 us)
Async XLA Ops:
  3.8 90.1 %collective-permute-start.16 = (bf16[3,32,4096]{2,1,0:T(8,128)(2,1)}, bf16[3,32,4096]{2,1,0:T(8,128)(2,1)}, u32[]{:S(2)}, u32[]{:S(2)}) collective-permute-start(bf16[3,32,4096]{2,1,0:T(8,128)(2,1)} %get-tuple-element.4), channel_id=1, source_target_pairs={{4,0},{12,8},{20,16},{8,12},{16,20},{24,28},{5,1},{13,9},{21,17},{... | collective-permute-start | bytes 2359304 | tf_op jit(solution)/shard_map/ppermute | solution.py:241
  7.2 29.3 %collective-permute-start = (bf16[1,32,8192]{2,1,0:T(8,128)(2,1)S(1)}, bf16[1,32,8192]{2,1,0:T(8,128)(2,1)S(1)}, u32[]{:S(2)}, u32[]{:S(2)}) collective-permute-start(bf16[1,32,8192]{2,1,0:T(8,128)(2,1)S(1)} %get-tuple-element.9), channel_id=1, source_target_pairs={{0,4},{4,8},{8,12},{12,16},{16,20},{20,24},{24,28},{1,5},{5,9},{9,... | collective-permute-start | bytes 1572872 | tf_op jit(solution)/shard_map/ppermute | solution.py:212
  12.9 26.0 %collective-permute-start.1 = (bf16[1,32,8192]{2,1,0:T(8,128)(2,1)}, bf16[1,32,8192]{2,1,0:T(8,128)(2,1)S(1)}, u32[]{:S(2)}, u32[]{:S(2)}) collective-permute-start(bf16[1,32,8192]{2,1,0:T(8,128)(2,1)} %get-tuple-element.8), channel_id=1, source_target_pairs={{4,0},{8,4},{12,8},{16,12},{20,16},{24,20},{28,24},{5,1},{9,5},{13... | collective-permute-start | bytes 1572872 | tf_op jit(solution)/shard_map/ppermute | solution.py:213
  15.9 53.7 %collective-permute-start.15 = (bf16[2,32,4096]{2,1,0:T(8,128)(2,1)S(1)}, bf16[2,32,4096]{2,1,0:T(8,128)(2,1)S(1)}, u32[]{:S(2)}, u32[]{:S(2)}) collective-permute-start(bf16[2,32,4096]{2,1,0:T(8,128)(2,1)S(1)} %get-tuple-element.6), channel_id=1, source_target_pairs={{0,4},{8,12},{16,20},{24,28},{4,0},{12,8},{20,16},{28,24},{1,5},{9... | collective-permute-start | bytes 1572872 | tf_op jit(solution)/shard_map/ppermute | solution.py:242
  19.3 78.9 %collective-permute-start.13 = (bf16[3,32,4096]{2,1,0:T(8,128)(2,1)}, bf16[3,32,4096]{2,1,0:T(8,128)(2,1)}, u32[]{:S(2)}, u32[]{:S(2)}) collective-permute-start(bf16[3,32,4096]{2,1,0:T(8,128)(2,1)} %get-tuple-element.5), channel_id=1, source_target_pairs={{4,0},{12,8},{16,20},{24,28},{5,1},{13,9},{17,21},{25,29},{6,2},{1... | collective-permute-start | bytes 2359304 | tf_op jit(solution)/shard_map/ppermute | solution.py:241
  36.4 40.7 %collective-permute-start.11 = (bf16[2,32,4096]{2,1,0:T(8,128)(2,1)S(1)}, bf16[2,32,4096]{2,1,0:T(8,128)(2,1)S(1)}, u32[]{:S(2)}, u32[]{:S(2)}) collective-permute-start(bf16[2,32,4096]{2,1,0:T(8,128)(2,1)S(1)} %get-tuple-element.7), channel_id=1, source_target_pairs={{0,4},{8,12},{16,20},{24,28},{4,0},{12,8},{20,16},{28,24},{1,5},{9... | collective-permute-start | bytes 1572872 | tf_op jit(solution)/shard_map/ppermute | solution.py:242
  48.9 15.7 %collective-permute-start.2 = (f32[65]{0:T(128)S(1)}, f32[65]{0:T(128)S(1)}, u32[]{:S(2)}, u32[]{:S(2)}) collective-permute-start(f32[65]{0:T(128)S(1)} %dynamic_update_slice.5), channel_id=1, source_target_pairs={{0,24},{8,0},{16,8},{24,16},{4,12},{12,20},{20,28},{28,4},{1,25},{... | collective-permute-start | bytes 788 | tf_op jit(solution)/shard_map/ppermute | solution.py:264
  64.7 5.5 %collective-permute-start.3 = (f32[65]{0:T(128)S(1)}, f32[65]{0:T(128)S(1)}, u32[]{:S(2)}, u32[]{:S(2)}) collective-permute-start(f32[65]{0:T(128)S(1)} %add_dynamic-update-slice_fusion), channel_id=1, source_target_pairs={{0,16},{8,24},{16,0},{24,8},{4,20},{12,28},{20,4},{28,12},{1,17},{... | collective-permute-start | bytes 788 | tf_op jit(solution)/shard_map/ppermute | solution.py:264
  69.5 40.5 %collective-permute-start.12 = (bf16[3,32,4096]{2,1,0:T(8,128)(2,1)}, bf16[3,32,4096]{2,1,0:T(8,128)(2,1)S(1)}, u32[]{:S(2)}, u32[]{:S(2)}) collective-permute-start(bf16[3,32,4096]{2,1,0:T(8,128)(2,1)} %get-tuple-element.5), channel_id=1, source_target_pairs={{20,24},{8,4},{21,25},{9,5},{22,26},{10,6},{23,27},{11,7}} | collective-permute-start | bytes 2359304 | tf_op jit(solution)/shard_map/ppermute | solution.py:245
  70.2 41.4 %collective-permute-start.9 = (bf16[2,32,6144]{2,1,0:T(8,128)(2,1)}, bf16[2,32,6144]{2,1,0:T(8,128)(2,1)}, u32[]{:S(2)}, u32[]{:S(2)}) collective-permute-start(bf16[2,32,6144]{2,1,0:T(8,128)(2,1)} %slice_select_fusion.3), channel_id=1, source_target_pairs={{4,0},{24,28},{5,1},{25,29},{6,2},{26,30},{7,3},{27,31}} | collective-permute-start | bytes 2359304 | tf_op jit(solution)/shard_map/ppermute | solution.py:241
  72.2 11.9 %copy-start.5 = (f32[65]{0:T(128)}, f32[65]{0:T(128)S(1)}, u32[]{:S(2)}) copy-start(f32[65]{0:T(128)S(1)} %add.40) | copy-start | bytes 784
  77.2 0.8 copy-start.1
  78.0 7.3 %collective-permute-start.4 = (f32[65]{0:T(128)S(1)}, f32[65]{0:T(128)}, u32[]{:S(2)}, u32[]{:S(2)}) collective-permute-start(f32[65]{0:T(128)S(1)} %add.40), channel_id=1, source_target_pairs={{0,28},{8,4},{16,12},{24,20},{4,8},{12,16},{20,24},{28,0},{1,29},{... | collective-permute-start | bytes 788 | tf_op jit(solution)/shard_map/ppermute | solution.py:268
  85.3 66.1 %collective-permute-start.7 = (bf16[3,32,6144]{2,1,0:T(8,128)(2,1)}, bf16[3,32,6144]{2,1,0:T(8,128)(2,1)S(1)}, u32[]{:S(2)}, u32[]{:S(2)}) collective-permute-start(bf16[3,32,6144]{2,1,0:T(8,128)(2,1)} %slice_select_fusion), channel_id=1, source_target_pairs={{0,4},{8,12},{16,20},{24,28},{4,0},{12,8},{20,16},{28,24},{1,5},{9... | collective-permute-start | bytes 3538952 | tf_op jit(solution)/shard_map/ppermute | solution.py:242
  93.9 22.4 %collective-permute-start.17 = (bf16[3,32,4096]{2,1,0:T(8,128)(2,1)}, bf16[3,32,4096]{2,1,0:T(8,128)(2,1)}, u32[]{:S(2)}, u32[]{:S(2)}) collective-permute-start(bf16[3,32,4096]{2,1,0:T(8,128)(2,1)} %collective-permute-done.16), channel_id=1, source_target_pairs={{0,8},{8,16},{16,24},{12,4},{20,12},{28,20},{1,9},{9,17},{17,25},{... | collective-permute-start | bytes 2359304 | tf_op jit(solution)/shard_map/ppermute | solution.py:247
  98.2 34.2 %collective-permute-start.14 = (bf16[3,32,4096]{2,1,0:T(8,128)(2,1)}, bf16[3,32,4096]{2,1,0:T(8,128)(2,1)}, u32[]{:S(2)}, u32[]{:S(2)}) collective-permute-start(bf16[3,32,4096]{2,1,0:T(8,128)(2,1)} %collective-permute-done.13), channel_id=1, source_target_pairs={{0,8},{8,16},{20,12},{28,20},{1,9},{9,17},{21,13},{29,21},{2,10},{... | collective-permute-start | bytes 2359304 | tf_op jit(solution)/shard_map/ppermute | solution.py:247
  106.2 0.5 copy-start.6
  110.1 41.3 %collective-permute-start.8 = (bf16[2,32,6144]{2,1,0:T(8,128)(2,1)}, bf16[2,32,6144]{2,1,0:T(8,128)(2,1)}, u32[]{:S(2)}, u32[]{:S(2)}) collective-permute-start(bf16[2,32,6144]{2,1,0:T(8,128)(2,1)} %slice_select_fusion.3), channel_id=1, source_target_pairs={{12,16},{20,24},{8,4},{16,12},{13,17},{21,25},{9,5},{17,13},{14,18... | collective-permute-start | bytes 2359304 | tf_op jit(solution)/shard_map/ppermute | solution.py:245
  111.6 39.7 %collective-permute-start.10 = (bf16[2,32,6144]{2,1,0:T(8,128)(2,1)}, bf16[2,32,6144]{2,1,0:T(8,128)(2,1)}, u32[]{:S(2)}, u32[]{:S(2)}) collective-permute-start(bf16[2,32,6144]{2,1,0:T(8,128)(2,1)} %collective-permute-done.9), channel_id=1, source_target_pairs={{0,8},{28,20},{1,9},{29,21},{2,10},{30,22},{3,11},{31,23}} | collective-permute-start | bytes 2359304 | tf_op jit(solution)/shard_map/ppermute | solution.py:247
  116.3 39.4 %collective-permute-start.5 = (bf16[3,32,2048]{2,1,0:T(8,128)(2,1)}, bf16[3,32,2048]{2,1,0:T(8,128)(2,1)}, u32[]{:S(2)}, u32[]{:S(2)}) collective-permute-start(bf16[3,32,2048]{2,1,0:T(8,128)(2,1)} %slice_select_fusion.6), channel_id=1, source_target_pairs={{0,4},{8,12},{16,20},{24,28},{4,0},{12,8},{20,16},{28,24},{1,5},{9... | collective-permute-start | bytes 1179656 | tf_op jit(solution)/shard_map/ppermute | solution.py:242
  116.4 17.4 %copy-start.4 = (f32[64]{0:T(128)}, f32[64]{0:T(128)S(1)}, u32[]{:S(2)}) copy-start(f32[64]{0:T(128)S(1)} %pad_maximum_fusion.1) | copy-start | bytes 772
  132.4 23.3 %collective-permute-start.6 = (bf16[2,32,2048]{2,1,0:T(8,128)(2,1)}, bf16[2,32,2048]{2,1,0:T(8,128)(2,1)}, u32[]{:S(2)}, u32[]{:S(2)}) collective-permute-start(bf16[2,32,2048]{2,1,0:T(8,128)(2,1)} %slice_select_fusion.7), channel_id=1, source_target_pairs={{4,8},{12,16},{20,24},{8,4},{16,12},{24,20},{5,9},{13,17},{21,25},... | collective-permute-start | bytes 786440 | tf_op jit(solution)/shard_map/ppermute | solution.py:245
  140.2 3.4 %copy-start = (bf16[8,32,16384]{2,1,0:T(8,128)(2,1)S(1)}, bf16[8,32,16384]{2,1,0:T(8,128)(2,1)}, u32[]{:S(2)}) copy-start(bf16[8,32,16384]{2,1,0:T(8,128)(2,1)} %points.7) | copy-start | bytes 25165828
  143.6 0.6 copy-start.3
  144.2 3.9 %copy-start.2 = (bf16[2,32,4096]{2,1,0:T(8,128)(2,1)S(1)}, bf16[2,32,4096]{2,1,0:T(8,128)(2,1)}, u32[]{:S(2)}) copy-start(bf16[2,32,4096]{2,1,0:T(8,128)(2,1)} %copy-done.1) | copy-start | bytes 1572868
  144.2 7.2 %slice-start = ((s8[8388608]{0:T(1024)(128)(4,1)}), s8[4194304]{0:T(1024)(128)(4,1)S(1)}, s32[]{:S(2)}) async-start(s8[8388608]{0:T(1024)(128)(4,1)} %bitcast.13), calls=%async_computation | async-start | bytes 8388608
  148.1 3.3 %slice-start.1 = ((s8[8388608]{0:T(1024)(128)(4,1)}), s8[4194304]{0:T(1024)(128)(4,1)S(1)}, s32[]{:S(2)}) async-start(s8[8388608]{0:T(1024)(128)(4,1)} %bitcast.13), calls=%async_computation.1 | async-start | bytes 8388608
